TPU v7x, 32 devices: a whole 2x2x4 slice. The times are simulated.
32 devices in a mesh: grp: 4 (over y, x), dp: 8 (over z, core).
Axes of the slice: x: 2, y: 2, z: 4, core: 2. Of those that a mesh axis runs over, the one named last changes fastest.
Arguments:
- byte_tokens: int32 [32, 2, 128], P(('grp', 'dp')), may hold values from 0 to 383
- seg_lengths: int32 [32, 2, 3], P(('grp', 'dp')), may hold values from 1 to 64, 128 in all within a row
- scripts: int32 [32, 2, 3], P(('grp', 'dp')), may hold values from 0 to 2
- routes: int32 [32, 2, 128, 1], P(('grp', 'dp')), may hold values from 0 to 7; in each aligned block of 128 rows (0 to 127, 128 to 255, ..., all dimensions but the last counted through in order) at most 24 rows name the same one
- step_count: int32 [1], replicated, may hold values from 2 to 20
- attention_in: float32 [3, 1536, 2304], P(None, 'dp'), may hold values from -0.15625 to 0.15625
- attention_out: float32 [3, 768, 1536], P(None, 'dp'), may hold values from -1.25 to 1.25
- feed_in: float32 [2, 1536, 7936], P(None, 'dp'), may hold values from -0.15625 to 0.15625
- feed_out: float32 [2, 3968, 1536], P(None, 'dp'), may hold values from -0.09375 to 0.09375
- embedding: float32 [384, 1536], P('dp'), may hold values from -6 to 6
- norm_gains: float32 [7, 1536], P(None, 'dp'), may hold values from 0.5 to 1.5
- first_attention_in: float32 [3, 1536, 2304], P(None, 'dp'), may hold values from -9.536743e-07 to 9.536743e-07
- first_attention_out: float32 [3, 768, 1536], P(None, 'dp'), may hold values from -9.536743e-07 to 9.536743e-07
- first_feed_in: float32 [2, 1536, 7936], P(None, 'dp'), may hold values from -9.536743e-07 to 9.536743e-07
- first_feed_out: float32 [2, 3968, 1536], P(None, 'dp'), may hold values from -9.536743e-07 to 9.536743e-07
- first_embedding: float32 [384, 1536], P('dp'), may hold values from -9.536743e-07 to 9.536743e-07
- first_norm_gains: float32 [7, 1536], P(None, 'dp'), may hold values from -9.536743e-07 to 9.536743e-07
- second_attention_in: float32 [3, 1536, 2304], P(None, 'dp'), may hold values from 9.741758e-16 to 1.5586812e-14
- second_attention_out: float32 [3, 768, 1536], P(None, 'dp'), may hold values from 9.741758e-16 to 1.5586812e-14
- second_feed_in: float32 [2, 1536, 7936], P(None, 'dp'), may hold values from 9.741758e-16 to 1.5586812e-14
- second_feed_out: float32 [2, 3968, 1536], P(None, 'dp'), may hold values from 9.741758e-16 to 1.5586812e-14
- second_embedding: float32 [384, 1536], P('dp'), may hold values from 9.741758e-16 to 1.5586812e-14
- second_norm_gains: float32 [7, 1536], P(None, 'dp'), may hold values from 9.741758e-16 to 1.5586812e-14
Outputs:
- new_attention_in: float32 [3, 1536, 2304], P(None, 'dp')
- new_attention_out: float32 [3, 768, 1536], P(None, 'dp')
- new_feed_in: float32 [2, 1536, 7936], P(None, 'dp')
- new_feed_out: float32 [2, 3968, 1536], P(None, 'dp')
- new_embedding: float32 [384, 1536], P('dp')
- new_norm_gains: float32 [7, 1536], P(None, 'dp')
- new_first_attention_in: float32 [3, 1536, 2304], P(None, 'dp')
- new_first_attention_out: float32 [3, 768, 1536], P(None, 'dp')
- new_first_feed_in: float32 [2, 1536, 7936], P(None, 'dp')
- new_first_feed_out: float32 [2, 3968, 1536], P(None, 'dp')
- new_first_embedding: float32 [384, 1536], P('dp')
- new_first_norm_gains: float32 [7, 1536], P(None, 'dp')
- new_second_attention_in: float32 [3, 1536, 2304], P(None, 'dp')
- new_second_attention_out: float32 [3, 768, 1536], P(None, 'dp')
- new_second_feed_in: float32 [2, 1536, 7936], P(None, 'dp')
- new_second_feed_out: float32 [2, 3968, 1536], P(None, 'dp')
- new_second_embedding: float32 [384, 1536], P('dp')
- new_second_norm_gains: float32 [7, 1536], P(None, 'dp')
- mean_loss: float32 [], replicated
- script_counts: float32 [3], replicated
- gradient_norm: float32 [], replicated
Inputs may be any that keep to these rules, and one draw needn't show every extreme that they name: `routes`: in each device's micro-batch at most 24 encoder rows name one decoder device, and some decoder device is named by exactly 24. `seg_lengths`: the 3 lengths of one device's micro-batch sum to 128; the longest is 64.
All inputs are finite; a program needn't handle non-finite values.
Results may differ from a plain program's by a relative error of at most 0.003.
The roundings to bfloat16 on the way count: a program that leaves them out, or rounds other values in their place, can miss the bound.
Values may be sent and summed in bfloat16 or wider, within the bound.
No kernel may reach another device: no remote copies, remote signals or barrier semaphores. Data moves between devices by JAX's collectives and lax.ppermute only.
A program may use at most 896 MiB of HBM per device.

v0:
```python
import jax
import jax.numpy as jnp
from jax import lax
from jax.sharding import PartitionSpec as P

HEADS = 12
HEAD_DIM = 64


LOW = jnp.bfloat16
FULL = jnp.float32
NORM_EPS = 1e-06
MASKED = -1e30
CLIP = 0.01
LEARN_RATE = 0.05
BETA_ONE = 0.9
BETA_TWO = 0.999
ADAM_EPS = 1e-08
DECAY = 0.01


def matmul(left, right):
    return jnp.dot(left, right, preferred_element_type=FULL)


def transposed_left(left, right):
    return lax.dot_general(left, right, (((0,), (0,)), ((), ())), preferred_element_type=FULL)


def transposed_right(left, right):
    return lax.dot_general(left, right, (((1,), (1,)), ((), ())), preferred_element_type=FULL)


def root_norm(stream, gain):
    return stream * lax.rsqrt(jnp.mean(stream * stream, -1, keepdims=True) + NORM_EPS) * gain


def root_norm_back(stream, gain, cotangent):
    unused, pull = jax.vjp(root_norm, stream, gain)
    return pull(cotangent)


def gate_apply(hidden):
    half_width = hidden.shape[1] // 2
    return jax.nn.gelu(hidden[:, :half_width], approximate=True) * hidden[:, half_width:]


def segment_of(lengths, row_count):
    bounds = jnp.cumsum(lengths)
    position = jnp.arange(row_count, dtype=jnp.int32)
    return jnp.sum((position[:, None] >= bounds[None, :]).astype(jnp.int32), 1)


def heads_of(matrix):
    return matrix.reshape(matrix.shape[0], HEADS, HEAD_DIM)


def lookup_back(inputs, cotangent, vocab_size):
    onehot = (inputs[:, None] == jnp.arange(vocab_size)[None, :]).astype(FULL)
    return lax.dot_general(
        onehot,
        cotangent,
        (((0,), (0,)), ((), ())),
        precision=lax.Precision.HIGHEST,
        preferred_element_type=FULL,
    )


def attend(queries, keys, values, allowed):
    scores = (
        jnp.einsum("qhd,khd->hqk", heads_of(queries), heads_of(keys), preferred_element_type=FULL)
        * 0.125
    )
    scores = jnp.where(allowed[None], scores, MASKED)
    row_max = jnp.max(scores, -1, keepdims=True)
    raised = jnp.exp(scores - row_max)
    shares = raised / jnp.sum(raised, -1, keepdims=True)
    attended = jnp.einsum(
        "hqk,khd->qhd", shares.astype(LOW), heads_of(values), preferred_element_type=FULL
    )
    return (attended.reshape(queries.shape[0], queries.shape[1]).astype(LOW), shares)


def attend_back(queries, keys, values, shares, grad_attended):
    grad_heads = heads_of(grad_attended)
    grad_shares = jnp.einsum(
        "qhd,khd->hqk", grad_heads, heads_of(values), preferred_element_type=FULL
    )
    grad_scores = shares * (grad_shares - jnp.sum(shares * grad_shares, -1, keepdims=True))
    grad_low = (grad_scores * 0.125).astype(LOW)
    grad_q = jnp.einsum("hqk,khd->qhd", grad_low, heads_of(keys), preferred_element_type=FULL)
    grad_k = jnp.einsum("hqk,qhd->khd", grad_low, heads_of(queries), preferred_element_type=FULL)
    grad_v = jnp.einsum("hqk,qhd->khd", shares.astype(LOW), grad_heads, preferred_element_type=FULL)
    return (grad_q.reshape(queries.shape), grad_k.reshape(keys.shape), grad_v.reshape(values.shape))


def self_forward(stream, gain, w_in, w_out, allowed):
    normed = root_norm(stream, gain).astype(LOW)
    packed = matmul(normed, w_in).astype(LOW)
    inner_width = packed.shape[1] // 3
    attended, shares = attend(
        packed[:, :inner_width],
        packed[:, inner_width : 2 * inner_width],
        packed[:, 2 * inner_width :],
        allowed,
    )
    return (stream + matmul(attended, w_out), (stream, normed, packed, attended, shares))


def self_backward(kept, gain, w_in, w_out, cotangent):
    stream, normed, packed, attended, shares = kept
    inner_width = packed.shape[1] // 3
    grad_low = cotangent.astype(LOW)
    grad_out = transposed_left(attended, grad_low)
    grad_attended = transposed_right(grad_low, w_out).astype(LOW)
    grad_q, grad_k, grad_v = attend_back(
        packed[:, :inner_width],
        packed[:, inner_width : 2 * inner_width],
        packed[:, 2 * inner_width :],
        shares,
        grad_attended,
    )
    grad_packed = jnp.concatenate([grad_q, grad_k, grad_v], 1).astype(LOW)
    grad_in = transposed_left(normed, grad_packed)
    grad_stream, grad_gain = root_norm_back(stream, gain, transposed_right(grad_packed, w_in))
    return (cotangent + grad_stream, grad_gain, grad_in, grad_out)


def feed_forward(stream, gain, w_in, w_out):
    normed = root_norm(stream, gain).astype(LOW)
    hidden = matmul(normed, w_in)
    gated = gate_apply(hidden).astype(LOW)
    return (stream + matmul(gated, w_out), (stream, normed, hidden, gated))


def feed_backward(kept, gain, w_in, w_out, cotangent):
    stream, normed, hidden, gated = kept
    grad_low = cotangent.astype(LOW)
    grad_out = transposed_left(gated, grad_low)
    unused, pull = jax.vjp(gate_apply, hidden)
    grad_hidden = pull(transposed_right(grad_low, w_out))[0].astype(LOW)
    grad_in = transposed_left(normed, grad_hidden)
    grad_stream, grad_gain = root_norm_back(stream, gain, transposed_right(grad_hidden, w_in))
    return (cotangent + grad_stream, grad_gain, grad_in, grad_out)


def run_role(active, worker, totals, *operands):
    probe = worker(totals, *operands)[1]
    blanks = jax.tree.map(lambda member: jnp.zeros(member.shape, member.dtype), probe)

    def skipped(totals, *unused):
        return (totals, blanks)

    return lax.cond(active, worker, skipped, totals, *operands)


def encode_forward(totals, tokens, lengths, weights):
    self_in, self_out, cross_in, cross_out, feed_in, feed_out, table, gains = weights
    segment = segment_of(lengths, tokens.shape[0])
    stream = jnp.take(table, tokens, axis=0).astype(FULL)
    stream, kept_self = self_forward(
        stream, gains[0], self_in, self_out, segment[:, None] == segment[None, :]
    )
    stream, kept_feed = feed_forward(stream, gains[1], feed_in, feed_out)
    final = root_norm(stream, gains[2]).astype(LOW)
    return (totals, (final, (kept_self, kept_feed, stream, final)))


def encode_backward(totals, kept, grad_rows, tokens, weights):
    self_in, self_out, cross_in, cross_out, feed_in, feed_out, table, gains = weights
    (
        total_self_in,
        total_self_out,
        total_cross_in,
        total_cross_out,
        total_feed_in,
        total_feed_out,
        total_table,
        total_gains,
    ) = totals
    kept_self, kept_feed, stream, final = kept
    cotangent, gain_two = root_norm_back(stream, gains[2], grad_rows)
    cotangent, gain_one, grad_feed_in, grad_feed_out = feed_backward(
        kept_feed, gains[1], feed_in, feed_out, cotangent
    )
    cotangent, gain_zero, grad_self_in, grad_self_out = self_backward(
        kept_self, gains[0], self_in, self_out, cotangent
    )
    totals = (
        total_self_in + grad_self_in,
        total_self_out + grad_self_out,
        total_cross_in,
        total_cross_out,
        total_feed_in + grad_feed_in,
        total_feed_out + grad_feed_out,
        total_table + lookup_back(tokens, cotangent, table.shape[0]),
        total_gains.at[0:3].add(jnp.stack([gain_zero, gain_one, gain_two])),
    )
    return (totals, jnp.zeros((), FULL))


def decode_step(totals, tokens, lengths, script_ids, memory, present, weights, scale_kind):
    self_in, self_out, cross_in, cross_out, feed_in, feed_out, table, gains = weights
    (
        total_self_in,
        total_self_out,
        total_cross_in,
        total_cross_out,
        total_feed_in,
        total_feed_out,
        total_table,
        total_gains,
    ) = totals
    row_count = tokens.shape[0]
    inner_width = cross_in.shape[1] // 3
    vocab_size = table.shape[0]
    scale_head = table.shape[1] ** (-0.5)
    segment = segment_of(lengths, row_count)
    position = jnp.arange(row_count, dtype=jnp.int32)
    starts = jnp.concatenate([jnp.ones((1,), bool), segment[1:] != segment[:-1]])
    previous = jnp.concatenate([jnp.zeros((1,), jnp.int32), tokens[:-1]])
    inputs = jnp.where(starts, 0, previous)
    stream = jnp.take(table, inputs, axis=0).astype(FULL)
    causal = (segment[:, None] == segment[None, :]) & (position[None, :] <= position[:, None])
    stream, kept_self = self_forward(stream, gains[3], self_in, self_out, causal)
    cross_stream = stream
    normed = root_norm(stream, gains[4]).astype(LOW)
    queries = matmul(normed, cross_in[:, :inner_width]).astype(LOW)
    keys_values = matmul(memory, cross_in[:, inner_width:]).astype(LOW)
    allowed = jnp.broadcast_to(present[None, :] > 0, (row_count, present.shape[0]))
    attended, shares = attend(
        queries, keys_values[:, :inner_width], keys_values[:, inner_width:], allowed
    )
    stream = stream + matmul(attended, cross_out)
    stream, kept_feed = feed_forward(stream, gains[5], feed_in, feed_out)
    head_in = (root_norm(stream, gains[6]) * scale_head).astype(LOW)
    logits = transposed_right(head_in, table)
    row_max = jnp.max(logits, -1, keepdims=True)
    raised = jnp.exp(logits - row_max)
    row_total = jnp.sum(raised, -1, keepdims=True)
    onehot_vocab = (jnp.arange(vocab_size)[None, :] == tokens[:, None]).astype(FULL)
    log_total = row_max[:, 0] + jnp.log(row_total[:, 0])
    picked = jnp.sum(logits * onehot_vocab, 1)
    token_kind = jnp.sum(
        jnp.where(
            segment[:, None] == jnp.arange(lengths.shape[0])[None, :], script_ids[None, :], 0
        ),
        1,
    )
    weight = jnp.sum(
        jnp.where(token_kind[:, None] == jnp.arange(3)[None, :], scale_kind[None, :], 0.0), 1
    )
    loss_part = jnp.sum((log_total - picked) * weight)
    grad_logits = ((raised / row_total - onehot_vocab) * weight[:, None]).astype(LOW)
    grad_table = transposed_left(grad_logits, head_in)
    cotangent, gain_six = root_norm_back(stream, gains[6], matmul(grad_logits, table) * scale_head)
    cotangent, gain_five, grad_feed_in, grad_feed_out = feed_backward(
        kept_feed, gains[5], feed_in, feed_out, cotangent
    )
    grad_low = cotangent.astype(LOW)
    grad_cross_out = transposed_left(attended, grad_low)
    grad_attended = transposed_right(grad_low, cross_out).astype(LOW)
    grad_q, grad_k, grad_v = attend_back(
        queries, keys_values[:, :inner_width], keys_values[:, inner_width:], shares, grad_attended
    )
    grad_queries = grad_q.astype(LOW)
    grad_kv = jnp.concatenate([grad_k, grad_v], 1).astype(LOW)
    grad_cross_q = transposed_left(normed, grad_queries)
    grad_cross_kv = transposed_left(memory, grad_kv)
    back_rows = transposed_right(grad_kv, cross_in[:, inner_width:])
    grad_stream, gain_four = root_norm_back(
        cross_stream, gains[4], transposed_right(grad_queries, cross_in[:, :inner_width])
    )
    cotangent = cotangent + grad_stream
    cotangent, gain_three, grad_self_in, grad_self_out = self_backward(
        kept_self, gains[3], self_in, self_out, cotangent
    )
    totals = (
        total_self_in + grad_self_in,
        total_self_out + grad_self_out,
        total_cross_in + jnp.concatenate([grad_cross_q, grad_cross_kv], 1),
        total_cross_out + grad_cross_out,
        total_feed_in + grad_feed_in,
        total_feed_out + grad_feed_out,
        total_table + grad_table + lookup_back(inputs, cotangent, vocab_size),
        total_gains.at[3:7].add(jnp.stack([gain_three, gain_four, gain_five, gain_six])),
    )
    return (totals, (back_rows, loss_part))


def optimizer_step(weight, first_moment, second, gradient, factor, step_value, decay):
    gradient = gradient * factor
    first_moment = BETA_ONE * first_moment + (1.0 - BETA_ONE) * gradient
    second = BETA_TWO * second + (1.0 - BETA_TWO) * gradient * gradient
    fixed_first = first_moment / (1.0 - BETA_ONE**step_value)
    fixed_second = second / (1.0 - BETA_TWO**step_value)
    weight = weight - LEARN_RATE * (
        fixed_first / (jnp.sqrt(fixed_second) + ADAM_EPS) + decay * weight
    )
    return (weight, first_moment, second)


def per_device(
    byte_tokens,
    seg_lengths,
    scripts,
    routes,
    step_count,
    attention_in,
    attention_out,
    feed_in,
    feed_out,
    embedding,
    norm_gains,
    first_attention_in,
    first_attention_out,
    first_feed_in,
    first_feed_out,
    first_embedding,
    first_norm_gains,
    second_attention_in,
    second_attention_out,
    second_feed_in,
    second_feed_out,
    second_embedding,
    second_norm_gains,
):
    groups = lax.axis_size("grp")
    members = lax.axis_size("dp")
    is_decoder = lax.axis_index("grp") == groups - 1
    role_index = is_decoder.astype(jnp.int32)
    as_decoder = is_decoder.astype(FULL)
    as_encoder = 1.0 - as_decoder
    shard_self_in = lax.dynamic_index_in_dim(attention_in, role_index, 0, keepdims=False)
    shard_self_out = lax.dynamic_index_in_dim(attention_out, role_index, 0, keepdims=False)
    shard_feed_in = lax.dynamic_index_in_dim(feed_in, role_index, 0, keepdims=False)
    shard_feed_out = lax.dynamic_index_in_dim(feed_out, role_index, 0, keepdims=False)
    copies = (
        lax.all_gather(shard_self_in.astype(LOW), "dp", axis=0, tiled=True),
        lax.all_gather(shard_self_out.astype(LOW), "dp", axis=0, tiled=True),
        lax.all_gather(attention_in[2].astype(LOW), "dp", axis=0, tiled=True),
        lax.all_gather(attention_out[2].astype(LOW), "dp", axis=0, tiled=True),
        lax.all_gather(shard_feed_in.astype(LOW), "dp", axis=0, tiled=True),
        lax.all_gather(shard_feed_out.astype(LOW), "dp", axis=0, tiled=True),
        lax.all_gather(embedding.astype(LOW), "dp", axis=0, tiled=True),
        lax.all_gather(norm_gains.astype(LOW), "dp", axis=1, tiled=True),
    )
    weights = tuple(copies[:7]) + (copies[7].astype(FULL),)
    local_counts = (
        jnp.sum(
            jnp.where(scripts[0][..., None] == jnp.arange(3), seg_lengths[0][..., None], 0), (0, 1)
        ).astype(FULL)
        * as_decoder
    )
    counts = lax.psum(local_counts, ("grp", "dp"))
    scale_kind = 1.0 / (3.0 * jnp.maximum(counts, 1.0))
    blank_totals = tuple((jnp.zeros(member.shape, FULL) for member in weights))
    totals = blank_totals
    row_count = byte_tokens.shape[2]
    capacity = 3 * row_count // (2 * members)
    loss_total = jnp.zeros((), FULL)
    for micro_index in range(byte_tokens.shape[1]):
        tokens = byte_tokens[0, micro_index]
        lengths = seg_lengths[0, micro_index]
        totals, (rows_sent, kept) = run_role(
            jnp.logical_not(is_decoder), encode_forward, totals, tokens, lengths, weights
        )
        row_width = rows_sent.shape[1]
        target = routes[0, micro_index, :, 0]
        hit_table = (target[:, None] == jnp.arange(members)[None, :]).astype(jnp.int32)
        order_in = jnp.sum((jnp.cumsum(hit_table, 0) - 1) * hit_table, 1)
        slot_index = target * capacity + order_in
        outgoing = jnp.zeros((members * capacity, row_width), LOW).at[slot_index].set(rows_sent)
        mark_rows = jnp.zeros((members * capacity,), LOW).at[slot_index].set(as_encoder.astype(LOW))
        arrived, arrived_marks = (
            lax.all_to_all(
                outgoing.reshape(members, capacity, row_width),
                "dp",
                split_axis=0,
                concat_axis=0,
                tiled=True,
            ),
            lax.all_to_all(
                mark_rows.reshape(members, capacity), "dp", split_axis=0, concat_axis=0, tiled=True
            ),
        )
        pooled, pooled_marks = (
            lax.all_gather(arrived, "grp", axis=0, tiled=True),
            lax.all_gather(arrived_marks, "grp", axis=0, tiled=True),
        )
        memory = pooled[: (groups - 1) * members].reshape(-1, row_width)
        present = pooled_marks[: (groups - 1) * members].reshape(-1)
        totals, (back_rows, loss_part) = run_role(
            is_decoder,
            decode_step,
            totals,
            tokens,
            lengths,
            scripts[0, micro_index],
            memory,
            present,
            weights,
            scale_kind,
        )
        loss_total = loss_total + loss_part
        returned = jnp.concatenate(
            [
                back_rows.reshape((groups - 1) * members, capacity, row_width),
                jnp.zeros((members, capacity, row_width), back_rows.dtype),
            ],
            0,
        )
        homed_rows = lax.psum_scatter(
            returned.astype(jnp.bfloat16), "grp", scatter_dimension=0, tiled=True
        ).astype(jnp.float32)
        reached = lax.all_to_all(
            homed_rows.astype(jnp.bfloat16), "dp", split_axis=0, concat_axis=0, tiled=True
        ).astype(homed_rows.dtype)
        grad_rows = jnp.take(reached.reshape(members * capacity, row_width), slot_index, axis=0)
        totals, unused = run_role(
            jnp.logical_not(is_decoder), encode_backward, totals, kept, grad_rows, tokens, weights
        )
    (
        total_self_in,
        total_self_out,
        total_cross_in,
        total_cross_out,
        total_feed_in,
        total_feed_out,
        total_table,
        total_gains,
    ) = totals
    owned = (
        lax.psum_scatter(total_self_in, "dp", scatter_dimension=0, tiled=True),
        lax.psum_scatter(total_self_out, "dp", scatter_dimension=0, tiled=True),
        lax.psum_scatter(total_cross_in, "dp", scatter_dimension=0, tiled=True),
        lax.psum_scatter(total_cross_out, "dp", scatter_dimension=0, tiled=True),
        lax.psum_scatter(total_feed_in, "dp", scatter_dimension=0, tiled=True),
        lax.psum_scatter(total_feed_out, "dp", scatter_dimension=0, tiled=True),
        lax.psum_scatter(total_table, "dp", scatter_dimension=0, tiled=True),
        lax.psum_scatter(total_gains, "dp", scatter_dimension=1, tiled=True),
    )
    stacked_in = jnp.stack([owned[0] * as_encoder, owned[0] * as_decoder, owned[2]])
    stacked_out = jnp.stack([owned[1] * as_encoder, owned[1] * as_decoder, owned[3]])
    stacked_feed_in = jnp.stack([owned[4] * as_encoder, owned[4] * as_decoder])
    stacked_feed_out = jnp.stack([owned[5] * as_encoder, owned[5] * as_decoder])
    summed = lax.psum(
        (
            stacked_in,
            stacked_out,
            stacked_feed_in,
            stacked_feed_out,
            owned[6],
            owned[7],
            loss_total,
        ),
        "grp",
    )
    gradients = summed[:6]
    squares = sum((jnp.sum(member * member) for member in gradients))
    square_total, loss_value = lax.psum((squares, summed[6]), "dp")
    norm = jnp.sqrt(square_total)
    factor = jnp.minimum(1.0, CLIP / (norm + 1e-06))
    step_value = step_count[0].astype(FULL)
    masters = (attention_in, attention_out, feed_in, feed_out, embedding, norm_gains)
    firsts = (
        first_attention_in,
        first_attention_out,
        first_feed_in,
        first_feed_out,
        first_embedding,
        first_norm_gains,
    )
    seconds = (
        second_attention_in,
        second_attention_out,
        second_feed_in,
        second_feed_out,
        second_embedding,
        second_norm_gains,
    )
    decays = (DECAY, DECAY, DECAY, DECAY, DECAY, 0.0)
    results = [
        optimizer_step(
            masters[index],
            firsts[index],
            seconds[index],
            gradients[index],
            factor,
            step_value,
            decays[index],
        )
        for index in range(6)
    ]
    return (
        results[0][0],
        results[1][0],
        results[2][0],
        results[3][0],
        results[4][0],
        results[5][0],
        results[0][1],
        results[1][1],
        results[2][1],
        results[3][1],
        results[4][1],
        results[5][1],
        results[0][2],
        results[1][2],
        results[2][2],
        results[3][2],
        results[4][2],
        results[5][2],
        loss_value,
        counts,
        norm,
    )


def solution(mesh):
    in_specs = (
        P(("grp", "dp"), None, None),
        P(("grp", "dp"), None, None),
        P(("grp", "dp"), None, None),
        P(("grp", "dp"), None, None, None),
        P(),
        P(None, "dp", None),
        P(None, "dp", None),
        P(None, "dp", None),
        P(None, "dp", None),
        P("dp", None),
        P(None, "dp"),
        P(None, "dp", None),
        P(None, "dp", None),
        P(None, "dp", None),
        P(None, "dp", None),
        P("dp", None),
        P(None, "dp"),
        P(None, "dp", None),
        P(None, "dp", None),
        P(None, "dp", None),
        P(None, "dp", None),
        P("dp", None),
        P(None, "dp"),
    )
    out_specs = (
        P(None, "dp", None),
        P(None, "dp", None),
        P(None, "dp", None),
        P(None, "dp", None),
        P("dp", None),
        P(None, "dp"),
        P(None, "dp", None),
        P(None, "dp", None),
        P(None, "dp", None),
        P(None, "dp", None),
        P("dp", None),
        P(None, "dp"),
        P(None, "dp", None),
        P(None, "dp", None),
        P(None, "dp", None),
        P(None, "dp", None),
        P("dp", None),
        P(None, "dp"),
        P(),
        P(),
        P(),
    )
    return jax.shard_map(
        per_device, mesh=mesh, in_specs=in_specs, out_specs=out_specs, check_vma=False
    )
```

profile of v0, /device:TPU:0, one launch (start us, length us, event | category | flops | bytes accessed | tf_op | source)
XLA Modules:
  0.0 3488.8 jit_solution(9935721285881984097)
XLA Ops:
  42.4 26.9 all-gather.27.cloned.1.call-done
  69.3 72.6 %all-gather.25.cloned.1.call-done = bf16[1,1536,2304]{2,1,0:T(8,128)(2,1)} async-done(((bf16[1,192,2304]{2,1,0:T(8,128)(2,1)}), bf16[1,1536,2304]{2,1,0:T(8,128)(2,1)}) %all-gather.25.cloned.1.call-update) | async-done | bytes 7077904 | tf_op jit(solution)/shard_map/all_gather | solution.py:339
  141.9 114.2 %all-gather.31.cloned.1.call-done = bf16[1,3968,1536]{2,1,0:T(8,128)(2,1)} async-done(((bf16[1,496,1536]{2,1,0:T(8,128)(2,1)}), bf16[1,3968,1536]{2,1,0:T(8,128)(2,1)}) %all-gather.31.cloned.1.call-update) | async-done | bytes 12189712 | tf_op jit(solution)/shard_map/all_gather | solution.py:344
  256.1 213.8 %all-gather.29.cloned.1.call-done = bf16[1,1536,7936]{2,1,0:T(8,128)(2,1)} async-done(((bf16[1,192,7936]{2,1,0:T(8,128)(2,1)}), bf16[1,1536,7936]{2,1,0:T(8,128)(2,1)}) %all-gather.29.cloned.1.call-update) | async-done | bytes 24379408 | tf_op jit(solution)/shard_map/all_gather | solution.py:343
  469.9 51.7 %conditional.6 = (bf16[128,1536]{1,0:T(8,128)(2,1)}, f32[128,1536]{1,0:T(8,128)S(1)}, bf16[128,1536]{1,0:T(8,128)(2,1)S(1)}, bf16[128,2304]{1,0:T(8,128)(2,1)}, ...) conditional(s32[]{:T(128)} %convert_element_type.382, () %tuple.73, ...), branch_computations={%region_2.3_spmd, %region_3.12_spmd} | conditional | flops 5949542400 | bytes 129024128 | solution.py:154
  523.8 36.1 %all_to_all.46 = bf16[8,24,1536]{2,1,0:T(8,128)(2,1)} all-to-all(bf16[8,24,1536]{2,1,0:T(8,128)(2,1)S(1)} %bitcast.401), channel_id=1, replica_groups=mesh['grp'=4,'dp'=8] {'dp'}, dimensions={0} | all-to-all | bytes 1179648 | tf_op jit(solution)/shard_map/all_to_all | solution.py:376
  567.3 41.1 %psum.70 = f32[3]{0:T(128)S(1)} all-reduce(f32[3]{0:T(128)S(1)} %convert_multiply_fusion.10), channel_id=1, replica_groups=mesh['grp'=4,'dp'=8] {'grp','dp'}, use_global_device_ids=true, to_apply=%region_14.16 | all-reduce | flops 3 | bytes 24 | tf_op jit(solution)/shard_map/psum | solution.py:355
  636.8 57.2 %conditional.7 = (f32[1536,2304]{1,0:T(8,128)}, f32[768,1536]{1,0:T(8,128)}, f32[1536,2304]{0,1:T(8,128)}, f32[768,1536]{1,0:T(8,128)}, f32[1536,7936]{1,0:T(8,1...) conditional(s32[]{:T(128)} %convert_element_type.383, () %tuple.72, ...), branch_computations={%region_15.17_spmd, %region_16.44_spmd} | conditional | flops 29956247552 | bytes 586037440 | solution.py:154
  697.3 49.2 %conditional.9 = (bf16[128,1536]{1,0:T(8,128)(2,1)}, f32[128,1536]{1,0:T(8,128)}, bf16[128,1536]{1,0:T(8,128)(2,1)}, bf16[128,2304]{1,0:T(8,128)(2,1)}, bf16[128...) conditional(s32[]{:T(128)} %convert_element_type.382, () %tuple.79, ...), branch_computations={%region_58.61_spmd, %region_59.69_spmd} | conditional | flops 5949542400 | bytes 109363224 | solution.py:154
  779.4 89.9 %reduce-scatter.13.cloned.1.call-done = bf16[8,24,1536]{2,1,0:T(8,128)(2,1)} async-done(((bf16[32,24,1536]{2,1,0:T(8,128)(2,1)}), bf16[8,24,1536]{2,1,0:T(8,128)(2,1)}) %reduce-scatter.13.cloned.1.call-update) | async-done | bytes 589840 | tf_op jit(solution)/shard_map/reduce_scatter | solution.py:413
  895.3 237.1 %conditional.8 = (f32[1536,2304]{0,1:T(8,128)}, f32[768,1536]{0,1:T(8,128)}, f32[1536,7936]{0,1:T(8,128)}, f32[3968,1536]{0,1:T(8,128)}, f32[384,1536]{1,0:T(8,128)}, /*index=5*/f32[7,1536]{1,0:T(8,128)}) conditional(s32[]{:T(128)} %convert_element_type.382, (f32[1536,2304]{1,0:T(8,128)}, f32[768,1536]{1,0:T(8,128)}, f32[1536,7936]{1,0:T(8,128)}, ...), branch_computations={%region_44.47_spmd, %region_45.58_spmd} | conditional | flops 12838270976 | bytes 483917440 | solution.py:154
  1006.3 48.3 %copy.593 = f32[1536,7936]{0,1:T(8,128)} copy(f32[1536,7936]{1,0:T(8,128)} %get-tuple-element.1220) | data formatting | bytes 97517568 | tf_op jit(solution)/shard_map
  1054.6 33.1 bitcast_add_fusion
  1087.7 24.5 copy.594
  1132.4 99.6 %conditional.10 = (f32[1536,2304]{1,0:T(8,128)}, f32[768,1536]{1,0:T(8,128)}, f32[1536,2304]{0,1:T(8,128)}, f32[768,1536]{1,0:T(8,128)}, f32[1536,7936]{1,0:T(8,...) conditional(s32[]{:T(128)} %convert_element_type.383, ...), branch_computations={%region_69.72_spmd, %region_70.99_spmd} | conditional | flops 29984497664 | bytes 843817984 | solution.py:154
  1133.7 48.4 %copy.600 = f32[1536,7936]{1,0:T(8,128)} copy(f32[1536,7936]{0,1:T(8,128)} %get-tuple-element.1232) | data formatting | bytes 97517568 | tf_op jit(solution)/shard_map
  1182.1 24.5 copy.601
  1235.1 163.9 %reduce-scatter.15.cloned.1.call-done = bf16[8,24,1536]{2,1,0:T(8,128)(2,1)} async-done(((bf16[32,24,1536]{2,1,0:T(8,128)(2,1)}), bf16[8,24,1536]{2,1,0:T(8,128)(2,1)}) %reduce-scatter.15.cloned.1.call-update) | async-done | bytes 589840 | tf_op jit(solution)/shard_map/reduce_scatter | solution.py:413
  1423.4 312.5 %conditional.11 = (f32[384,1536]{1,0:T(8,128)}, f32[7,1536]{1,0:T(8,128)}, f32[1536,2304]{1,0:T(8,128)}, f32[768,1536]{1,0:T(8,128)}, f32[1536,7936]{1,0:T(8,128)}, /*index=5*/f32[3968,1536]{1,0:T(8,128)}) conditional(s32[]{:T(128)} %convert_element_type.382, (f32[1536,2304]{1,0:T(8,128)}, f32[768,1536]{1,0:T(8,128)}, f32[1536,7936]{1,0:T(8,128)}, ...), branch_computations={%region_98.101_spmd, %region_99.112_spmd} | conditional | flops 12838270976 | bytes 665818560 | solution.py:154
  1541.0 48.6 %copy.615 = f32[1536,7936]{0,1:T(8,128)} copy(f32[1536,7936]{1,0:T(8,128)} %get-tuple-element.1280) | data formatting | bytes 97517568 | tf_op jit(solution)/shard_map
  1589.6 32.3 bitcast_add_fusion.4
  1621.9 48.4 %copy.647 = f32[1536,7936]{1,0:T(8,128)} copy(f32[1536,7936]{0,1:T(8,128)} %bitcast_add_fusion.4) | data formatting | bytes 97517568 | tf_op jit(solution)/shard_map/cond | solution.py:154
  1670.3 24.5 copy.616
  1756.4 32.5 reduce-scatter.21.cloned.1.call-done
  1790.1 55.0 %reduce-scatter.23.cloned.1.call-done = f32[96,1536]{1,0:T(8,128)} async-done(((f32[768,1536]{1,0:T(8,128)}), f32[96,1536]{1,0:T(8,128)}) %reduce-scatter.23.cloned.1.call-update) | async-done | bytes 589840 | tf_op jit(solution)/shard_map/reduce_scatter | solution.py:437
  1847.5 142.2 %reduce-scatter.17.cloned.1.call-done = f32[192,2304]{1,0:T(8,128)} async-done(((f32[1536,2304]{1,0:T(8,128)}), f32[192,2304]{1,0:T(8,128)}) %reduce-scatter.17.cloned.1.call-update) | async-done | bytes 1769488 | tf_op jit(solution)/shard_map/reduce_scatter | solution.py:434
  1991.4 142.9 %reduce-scatter.19.cloned.1.call-done = f32[192,2304]{1,0:T(8,128)} async-done(((f32[1536,2304]{1,0:T(8,128)}), f32[192,2304]{1,0:T(8,128)}) %reduce-scatter.19.cloned.1.call-update) | async-done | bytes 1769488 | tf_op jit(solution)/shard_map/reduce_scatter | solution.py:436
  2138.5 236.2 %reduce-scatter.27.cloned.1.call-done = f32[496,1536]{1,0:T(8,128)} async-done(((f32[3968,1536]{1,0:T(8,128)}), f32[496,1536]{1,0:T(8,128)}) %reduce-scatter.27.cloned.1.call-update) | async-done | bytes 3047440 | tf_op jit(solution)/shard_map/reduce_scatter | solution.py:439
  2380.4 463.4 %reduce-scatter.25.cloned.1.call-done = f32[192,7936]{1,0:T(8,128)} async-done(((f32[1536,7936]{1,0:T(8,128)}), f32[192,7936]{1,0:T(8,128)}) %reduce-scatter.25.cloned.1.call-update) | async-done | bytes 6094864 | tf_op jit(solution)/shard_map/reduce_scatter | solution.py:438
  2881.9 32.9 reduce-scatter.31.cloned.1.call-done
  2927.2 446.9 %all-reduce.16.cloned.1.call-done = (f32[3,192,2304]{2,1,0:T(8,128)}, f32[3,96,1536]{2,1,0:T(8,128)}, f32[2,192,7936]{2,1,0:T(8,128)}, f32[2,496,1536]{2,1,0:T(8,128)}, f32[48,1536]{1,0:T(8,128)}) async-done(((f32[3,192,2304]{2,1,0:T(8,128)}, f32[3,96,1536]{2,1,0:T(8,128)}, f32[2,192,7936]{2,1,0:T(8,128)}, f32[2,496,1536]{2,1,0:T(8,128)}, f32[48,1536]{1,0:T(8,128)}), (f32[3,192,2304]{2,1,0:T(8,128)}, ...) | async-done | bytes 25657360 | tf_op jit(solution)/shard_map/psum | solution.py:447
  3431.2 31.5 multiply_subtract_fusion
  (393 shorter events, 778.7 us)
Async XLA Ops:
  7.2 35.2 %all-gather.19.cloned.1.call-start = ((), (), s32[]{:S(2)}) async-start(), calls=%async_computation.16 | async-start | bytes 1327104 | tf_op jit(solution)/shard_map/all_gather | solution.py:345
  8.9 60.4 %all-gather.27.cloned.1.call-start = ((), (), s32[]{:S(2)}) async-start(), calls=%async_computation.29 | async-start | bytes 2654208 | tf_op jit(solution)/shard_map/all_gather | solution.py:340
  11.1 130.8 %all-gather.25.cloned.1.call-start = ((), (), s32[]{:S(2)}) async-start(), calls=%async_computation.28 | async-start | bytes 7962624 | tf_op jit(solution)/shard_map/all_gather | solution.py:339
  14.6 241.5 %all-gather.31.cloned.1.call-start = ((), (), s32[]{:S(2)}) async-start(), calls=%async_computation.31 | async-start | bytes 13713408 | tf_op jit(solution)/shard_map/all_gather | solution.py:344
  17.8 452.0 %all-gather.29.cloned.1.call-start = ((), (), s32[]{:S(2)}) async-start(), calls=%async_computation.30 | async-start | bytes 27426816 | tf_op jit(solution)/shard_map/all_gather | solution.py:343
  22.7 595.9 %all-gather.35.cloned.1.call-start = ((), (), s32[]{:S(2)}) async-start(), calls=%async_computation.33 | async-start | bytes 2654208 | tf_op jit(solution)/shard_map/all_gather | solution.py:342
  23.2 595.3 %all-gather.33.cloned.1.call-start = ((), (), s32[]{:S(2)}) async-start(), calls=%async_computation.32 | async-start | bytes 7962624 | tf_op jit(solution)/shard_map/all_gather | solution.py:341
  24.0 612.8 %all-gather.21.cloned.1.call-start = ((), (), s32[]{:S(2)}) async-start(), calls=%async_computation.17 | async-start | bytes 2949120 | tf_op jit(solution)/shard_map/all_gather | solution.py:388
  39.9 429.9 %copy-start.89 = (f32[1536,7]{0,1:T(8,128)}, f32[1536,7]{0,1:T(8,128)S(1)}, u32[]{:S(2)}) copy-start(f32[1536,7]{0,1:T(8,128)S(1)} %reshape.1247) | copy-start | bytes 129028
  40.6 429.2 %copy-start.173 = (s32[128]{0:T(128)}, s32[128]{0:T(128)S(1)}, u32[]{:S(2)}) copy-start(s32[128]{0:T(128)S(1)} %get-tuple-element.1509) | copy-start | bytes 1540
  40.7 429.2 %copy-start.175 = (s32[128]{0:T(128)}, s32[128]{0:T(128)S(1)}, u32[]{:S(2)}) copy-start(s32[128]{0:T(128)S(1)} %get-tuple-element.1510) | copy-start | bytes 1540
  41.2 428.6 %copy-start.204 = (s32[128]{0:T(128)}, s32[128]{0:T(128)S(1)}, u32[]{:S(2)}) copy-start(s32[128]{0:T(128)S(1)} %get-tuple-element.1500) | copy-start | bytes 1540
  563.7 45.3 %all-to-all-start.1 = ((bf16[8,1,24]{2,1,0:T(2,128)(2,1)}), bf16[8,1,24]{2,1,0:T(2,128)(2,1)S(1)}, u32[]{:S(2)}, u32[]{:S(2)}) async-start(bf16[8,1,24]{2,1,0:T(2,128)(2,1)} %all_to_all.38), calls=%async_computation.1 | async-start | bytes 8192 | tf_op jit(solution)/shard_map/all_to_all | solution.py:383
  567.0 302.2 %reduce-scatter.13.cloned.1.call-start = ((), (), s32[]{:S(2)}) async-start(), calls=%async_computation.18 | async-start | bytes 2949120 | tf_op jit(solution)/shard_map/reduce_scatter | solution.py:413
  697.2 435.2 %all-gather.23.cloned.1.call-start = ((), (), s32[]{:S(2)}) async-start(), calls=%async_computation.19 | async-start | bytes 2949120 | tf_op jit(solution)/shard_map/all_gather | solution.py:388
  746.5 127.4 %copy-start.142 = (s32[1,2,128,1]{2,3,1,0:T(1,128)S(1)}, s32[1,2,128,1]{2,3,1,0:T(1,128)}, u32[]{:S(2)}) copy-start(s32[1,2,128,1]{2,3,1,0:T(1,128)} %param.50) | copy-start | bytes 3076
  746.5 127.4 %copy-start.174 = (s32[128]{0:T(128)S(1)}, s32[128]{0:T(128)}, u32[]{:S(2)}) copy-start(s32[128]{0:T(128)} %copy-done.173) | copy-start | bytes 1540
  746.5 127.4 %copy-start.176 = (s32[128]{0:T(128)S(1)}, s32[128]{0:T(128)}, u32[]{:S(2)}) copy-start(s32[128]{0:T(128)} %copy-done.175) | copy-start | bytes 1540
  869.3 21.5 all-to-all-start.2
  873.9 525.1 %reduce-scatter.15.cloned.1.call-start = ((), (), s32[]{:S(2)}) async-start(), calls=%async_computation.20 | async-start | bytes 2949120 | tf_op jit(solution)/shard_map/reduce_scatter | solution.py:413
  895.3 237.1 %copy-start.1 = (bf16[384,1536]{1,0:T(8,128)(2,1)S(1)}, bf16[384,1536]{1,0:T(8,128)(2,1)}, u32[]{:S(2)}) copy-start(bf16[384,1536]{1,0:T(8,128)(2,1)} %all-gather.19.cloned.1.call-done) | copy-start | bytes 3538948
  1232.0 171.6 %copy-start.157 = (s32[128]{0:T(128)S(1)}, s32[128]{0:T(128)}, u32[]{:S(2)}) copy-start(s32[128]{0:T(128)} %get-tuple-element.1497) | copy-start | bytes 1540
  1399.0 21.5 all-to-all-start.5
  1403.5 385.3 %reduce-scatter.21.cloned.1.call-start = ((), (), s32[]{:S(2)}) async-start(), calls=%async_computation.23 | async-start | bytes 5308416 | tf_op jit(solution)/shard_map/reduce_scatter | solution.py:435
  1735.9 109.2 %reduce-scatter.23.cloned.1.call-start = ((), (), s32[]{:S(2)}) async-start(), calls=%async_computation.24 | async-start | bytes 5308416 | tf_op jit(solution)/shard_map/reduce_scatter | solution.py:437
  1736.7 253.1 %reduce-scatter.17.cloned.1.call-start = ((), (), s32[]{:S(2)}) async-start(), calls=%async_computation.21 | async-start | bytes 15925248 | tf_op jit(solution)/shard_map/reduce_scatter | solution.py:434
  1737.2 397.1 %reduce-scatter.19.cloned.1.call-start = ((), (), s32[]{:S(2)}) async-start(), calls=%async_computation.22 | async-start | bytes 15925248 | tf_op jit(solution)/shard_map/reduce_scatter | solution.py:436
  1752.5 622.1 %reduce-scatter.27.cloned.1.call-start = ((), (), s32[]{:S(2)}) async-start(), calls=%async_computation.26 | async-start | bytes 27426816 | tf_op jit(solution)/shard_map/reduce_scatter | solution.py:439
  1753.1 1090.7 %reduce-scatter.25.cloned.1.call-start = ((), (), s32[]{:S(2)}) async-start(), calls=%async_computation.25 | async-start | bytes 54853632 | tf_op jit(solution)/shard_map/reduce_scatter | solution.py:438
  1753.7 1127.5 %reduce-scatter.29.cloned.1.call-start = ((), (), s32[]{:S(2)}) async-start(), calls=%async_computation.27 | async-start | bytes 2654208 | tf_op jit(solution)/shard_map/reduce_scatter | solution.py:440
  1754.3 1160.6 %reduce-scatter.31.cloned.1.call-start = ((), (), s32[]{:S(2)}) async-start(), calls=%async_computation.34 | async-start | bytes 884736
  1756.3 1617.7 %all-reduce.16.cloned.1.call-start = ((), (), s32[]{:S(2)}) async-start(), calls=%async_computation.35 | async-start | bytes 51314688 | tf_op jit(solution)/shard_map/psum | solution.py:447
  (54 other events, 858.2 us)
Sparse Core Ops, SparseCore 0:
  10.2 25.4 all-gather.18
  37.9 31.3 all-gather.26
  71.5 70.3 all-gather.24
  144.0 112.0 all-gather.30
  258.1 211.6 all-gather.28
  471.9 29.8 all-gather.34
  504.0 95.7 all-gather.32
  601.7 35.1 all-gather.20
  697.3 171.8 reduce-scatter.12
  871.0 37.5 all-gather.22
  1235.2 163.6 reduce-scatter.14
  1736.0 52.8 reduce-scatter.20
  1791.8 53.3 reduce-scatter.22
  1847.3 142.4 reduce-scatter.16
  1991.9 142.4 reduce-scatter.18
  2136.6 238.0 reduce-scatter.26
  2377.1 466.7 reduce-scatter.24
  2846.5 34.5 reduce-scatter.28
  2884.0 30.7 reduce-scatter.30
  2920.8 453.1 all-reduce.15
where the time goes:
time: 3500 us; the launch traced here: 3490 us
  waiting for transfers between devices  2300 us (66%)
  local copies, waits for them, and re-layouts  509 us (15%)
  matrix products  291 us (8%)
  blocking collectives  172 us (5%)
  other arithmetic  171 us (5%)
    reduce_scatter x1, waiting for transfers between devices, per_device(): lax.psum_scatter(total_feed_in, 'dp', scatter_dimension=0, tiled=True)  463 us
    psum x1, waiting for transfers between devices, per_device(): lax.psum((stacked_in, stacked_out, stacked_feed_in, stacked_feed_out, own...  447 us
    another operation x20, local copies, waits for them, and re-layouts  307 us
    reduce_scatter x2, waiting for transfers between devices, per_device(): lax.psum_scatter(returned.astype(jnp.bfloat16), 'grp', scatter_dimension=...  254 us
    reduce_scatter x1, waiting for transfers between devices, per_device(): lax.psum_scatter(total_feed_out, 'dp', scatter_dimension=0, tiled=True)  236 us
    all_gather x1, waiting for transfers between devices, per_device(): lax.all_gather(shard_feed_in.astype(LOW), 'dp', axis=0, tiled=True)  214 us
    reduce_scatter x1, waiting for transfers between devices, per_device(): lax.psum_scatter(total_cross_in, 'dp', scatter_dimension=0, tiled=True)  143 us
    reduce_scatter x1, waiting for transfers between devices, per_device(): lax.psum_scatter(total_self_in, 'dp', scatter_dimension=0, tiled=True)  142 us
  transfers between devices with their start and end apart: 23, of which 18 were waited for; matrix products, arithmetic and copies ran while one was open for 12% of the time, Pallas kernels for 0%

commit v1 on v0

v1 whole, which is shorter than its diff:
```python
import functools

import jax
import jax.numpy as jnp
from jax import lax
from jax.experimental import pallas as pl
from jax.experimental.pallas import tpu as pltpu
from jax.sharding import PartitionSpec as P

HEAD_DIM = 64
LANES = 128

LOW = jnp.bfloat16
FULL = jnp.float32
NORM_EPS = 1e-06
MASKED = -1e30
CLIP = 0.01
LEARN_RATE = 0.05
BETA_ONE = 0.9
BETA_TWO = 0.999
ADAM_EPS = 1e-08
DECAY = 0.01


def matmul(left, right):
    return jnp.dot(left, right, preferred_element_type=FULL)


def transposed_left(left, right):
    return lax.dot_general(left, right, (((0,), (0,)), ((), ())), preferred_element_type=FULL)


def transposed_right(left, right):
    return lax.dot_general(left, right, (((1,), (1,)), ((), ())), preferred_element_type=FULL)


def root_norm(stream, gain):
    return stream * lax.rsqrt(jnp.mean(stream * stream, -1, keepdims=True) + NORM_EPS) * gain


def root_norm_back(stream, gain, cotangent):
    unused, pull = jax.vjp(root_norm, stream, gain)
    return pull(cotangent)


def gate_apply(hidden):
    half_width = hidden.shape[1] // 2
    return jax.nn.gelu(hidden[:, :half_width], approximate=True) * hidden[:, half_width:]


def heads_of(matrix):
    return matrix.reshape(matrix.shape[0], matrix.shape[1], matrix.shape[2] // HEAD_DIM, HEAD_DIM)


def attend(queries, keys, values, allowed):
    scores = (
        jnp.einsum("bqhd,bkhd->bhqk", heads_of(queries), heads_of(keys), preferred_element_type=FULL)
        * 0.125
    )
    scores = jnp.where(allowed[:, None], scores, MASKED)
    row_max = jnp.max(scores, -1, keepdims=True)
    raised = jnp.exp(scores - row_max)
    shares = raised / jnp.sum(raised, -1, keepdims=True)
    attended = jnp.einsum(
        "bhqk,bkhd->bqhd", shares.astype(LOW), heads_of(values), preferred_element_type=FULL
    )
    return (attended.reshape(queries.shape).astype(LOW), shares)


def attend_back(queries, keys, values, shares, grad_attended):
    grad_heads = heads_of(grad_attended)
    grad_shares = jnp.einsum(
        "bqhd,bkhd->bhqk", grad_heads, heads_of(values), preferred_element_type=FULL
    )
    grad_scores = shares * (grad_shares - jnp.sum(shares * grad_shares, -1, keepdims=True))
    grad_low = (grad_scores * 0.125).astype(LOW)
    grad_q = jnp.einsum("bhqk,bkhd->bqhd", grad_low, heads_of(keys), preferred_element_type=FULL)
    grad_k = jnp.einsum("bhqk,bqhd->bkhd", grad_low, heads_of(queries), preferred_element_type=FULL)
    grad_v = jnp.einsum(
        "bhqk,bqhd->bkhd", shares.astype(LOW), grad_heads, preferred_element_type=FULL
    )
    return (
        grad_q.reshape(queries.shape).astype(LOW),
        grad_k.reshape(keys.shape).astype(LOW),
        grad_v.reshape(values.shape).astype(LOW),
    )


def adam(weight, first_moment, second, gradient, factor, fix_one, fix_two, decay):
    gradient = gradient * factor
    first_moment = BETA_ONE * first_moment + (1.0 - BETA_ONE) * gradient
    second = BETA_TWO * second + (1.0 - BETA_TWO) * gradient * gradient
    fixed_first = first_moment / fix_one
    fixed_second = second / fix_two
    weight = weight - LEARN_RATE * (
        fixed_first / (jnp.sqrt(fixed_second) + ADAM_EPS) + decay * weight
    )
    return (weight, first_moment, second)


def send(value, step, sources=None):
    groups = lax.axis_size("grp")
    sources = range(groups) if sources is None else sources
    return lax.ppermute(value, "grp", [(source, source ^ step) for source in sources])


def halves(value):
    middle = value.shape[1] // 2
    return value[:, :middle], value[:, middle:]


def gather_groups(value):
    rows = value.shape[0]
    left, right = halves(value)
    left_one = send(left, 1)
    right_two = send(right, 2)
    left_more = send(jnp.concatenate([left, left_one], 0), 2)
    right_more = send(jnp.concatenate([right, right_two], 0), 1)
    return jnp.concatenate(
        [
            jnp.concatenate([left, left_one, left_more], 0),
            jnp.concatenate([right, right_more[:rows], right_two, right_more[rows:]], 0),
        ],
        1,
    )


def reduce_groups(parts):
    rows = parts.shape[0] // 4
    left, right = halves(parts)
    left_low, right_low = left.astype(LOW), right.astype(LOW)
    got_left = send(left_low[2 * rows :], 2).astype(FULL)
    got_right = send(
        jnp.concatenate([right_low[rows : 2 * rows], right_low[3 * rows :]], 0), 1
    ).astype(FULL)
    more_left = send((left[rows : 2 * rows] + got_left[rows:]).astype(LOW), 1).astype(FULL)
    more_right = send((right[2 * rows : 3 * rows] + got_right[rows:]).astype(LOW), 2).astype(FULL)
    return jnp.concatenate(
        [left[:rows] + got_left[:rows] + more_left, right[:rows] + got_right[:rows] + more_right],
        1,
    )


def spread_last(value, is_last):
    last = lax.axis_size("grp") - 1
    left, right = halves(value)
    left_first = send(left, 1, [last])
    right_first = send(right, 2, [last])
    right_then = send(jnp.where(is_last, right, right_first), 1, [last, last ^ 2])
    left_then = send(jnp.where(is_last, left, left_first), 2, [last, last ^ 1])
    own = jnp.where(is_last, value, jnp.zeros_like(value))
    return own + jnp.concatenate([left_first + left_then, right_first + right_then], 1)


def collect_last(part):
    last = lax.axis_size("grp") - 1
    left, right = halves(part)
    left_first = send(left.astype(LOW), 2, [last ^ 3, last ^ 2]).astype(FULL)
    right_first = send(right.astype(LOW), 1, [last ^ 3, last ^ 1]).astype(FULL)
    left_then = send((left + left_first).astype(LOW), 1, [last ^ 1]).astype(FULL)
    right_then = send((right + right_first).astype(LOW), 2, [last ^ 2]).astype(FULL)
    return jnp.concatenate([left + left_first + left_then, right + right_first + right_then], 1)


def by_group(slots, group):
    return [
        lax.dynamic_index_in_dim(slots, group ^ source, 0, keepdims=False)
        for source in range(slots.shape[0])
    ]


def tie(value, *others):
    return lax.optimization_barrier((value,) + others)[0]


def deal_columns(feed_in, group, groups):
    layers, rows, width = feed_in.shape
    half = width // 2
    blocks = half // LANES
    own = -(-blocks // groups)

    def kernel(group_ref, source_ref, out_ref):
        place = pl.program_id(1) % own
        inside = groups * place + group_ref[0] < blocks
        out_ref[...] = jnp.where(inside, source_ref[...], 0.0).astype(LOW)

    def source_map(layer, step, group_ref):
        block = jnp.minimum(groups * (step % own) + group_ref[0], blocks - 1)
        return (layer, 0, (step // own) * blocks + block)

    return pl.pallas_call(
        kernel,
        out_shape=jax.ShapeDtypeStruct((layers, rows, 2 * own * LANES), LOW),
        grid_spec=pltpu.PrefetchScalarGridSpec(
            num_scalar_prefetch=1,
            grid=(layers, 2 * own),
            in_specs=[pl.BlockSpec((1, rows, LANES), source_map)],
            out_specs=pl.BlockSpec((1, rows, LANES), lambda layer, step, ref: (layer, 0, step)),
        ),
    )(group.reshape(1), feed_in)


class RowDeal:
    def __init__(self, shard_rows, members, groups):
        self.rows = shard_rows
        self.members = members
        self.groups = groups
        self.round = groups * LANES
        self.gap = self.round - shard_rows
        self.blocks = shard_rows * members // LANES
        self.own = -(-self.blocks // groups)
        self.snug = self.gap > 0 and self.gap * members == LANES and self.own == members

    def gather(self, shard, group, member):
        width = shard.shape[1]
        if not self.snug:
            whole = lax.all_gather(shard, "dp", axis=0, tiled=True)
            padded = jnp.pad(whole, ((0, self.own * self.round - whole.shape[0]), (0, 0)))
            dealt = padded.reshape(self.own, self.groups, LANES, width)
            picked = lax.dynamic_index_in_dim(dealt, group, 1, keepdims=False)
            return picked.reshape(self.own * LANES, width)
        padded = jnp.pad(shard, ((0, self.gap), (0, 0)))
        doubled = jnp.concatenate([padded, padded], 0)
        piece = lax.dynamic_slice(
            doubled, (self.gap * member + LANES * group, 0), (LANES, width)
        )
        held = lax.all_gather(piece, "dp", axis=0, tiled=False)
        after = jnp.concatenate([held[1:], jnp.zeros_like(held[:1])], 0)
        limit = (LANES - self.gap) - self.gap * jnp.arange(self.members)[:, None, None]
        place = jnp.arange(LANES)[None, :, None]
        wrapped = jnp.where(place < limit, held, after)
        return jnp.where(group == self.groups - 1, wrapped, held).reshape(-1, width)

    def arrange(self, grad, group):
        width = grad.shape[1]
        if not self.snug:
            spread = jnp.zeros((self.own, self.groups, LANES, width), grad.dtype)
            spread = lax.dynamic_update_index_in_dim(
                spread, grad.reshape(self.own, 1, LANES, width), group, 1
            )
            return spread.reshape(-1, width)[: self.rows * self.members]
        held = grad.reshape(self.members, LANES, width)
        before = jnp.concatenate([jnp.zeros_like(held[:1]), held[:-1]], 0)
        index = self.gap * jnp.arange(self.members)[:, None, None]
        place = jnp.arange(LANES)[None, :, None]
        wrapped = jnp.where(
            place < (LANES - self.gap) - index,
            held,
            jnp.where(place >= LANES - index, before, jnp.zeros_like(held)),
        )
        held = jnp.where(group == self.groups - 1, wrapped, held)
        return held.reshape(-1, width)

    def restore(self, parts, member):
        if not self.snug:
            return jnp.sum(parts, 0)
        width = parts.shape[2]
        line = parts.reshape(self.round, width)
        doubled = jnp.concatenate([line, line], 0)
        start = (self.round - self.gap * member) % self.round
        return lax.dynamic_slice(doubled, (start, 0), (self.rows, width))


def feed_in_step(weights, firsts, seconds, dealt, scalars, group):
    layers, rows, width = weights.shape
    groups = dealt[0].shape[0]
    blocks = width // LANES
    half_blocks = blocks // 2
    own = dealt[0].shape[2] // (2 * LANES)
    dealt = jnp.stack(dealt)

    def kernel(group_ref, scalar_ref, w_ref, m_ref, v_ref, *rest):
        grads, outs = rest[:groups], rest[groups:]
        for place in range(groups):
            lanes = slice(place * LANES, (place + 1) * LANES)
            gradient = grads[place][0, 0].astype(FULL)
            new = adam(
                w_ref[0, :, lanes],
                m_ref[0, :, lanes],
                v_ref[0, :, lanes],
                gradient,
                scalar_ref[0],
                scalar_ref[1],
                scalar_ref[2],
                DECAY,
            )
            for out, value in zip(outs, new):
                out[0, :, lanes] = value

    def grad_spec(place):
        def index(layer, step, group_ref, scalar_ref):
            block = jnp.minimum(step * groups + place, blocks - 1)
            part = (block >= half_blocks).astype(jnp.int32)
            block = block - part * half_blocks
            slot = jnp.bitwise_xor(group_ref[0], block % groups)
            return (layer, slot, 0, part * own + block // groups)

        return pl.BlockSpec((1, 1, rows, LANES), index)

    state_spec = pl.BlockSpec(
        (1, rows, groups * LANES), lambda layer, step, group_ref, scalar_ref: (layer, 0, step)
    )
    return pl.pallas_call(
        kernel,
        out_shape=[jax.ShapeDtypeStruct(weights.shape, FULL)] * 3,
        grid_spec=pltpu.PrefetchScalarGridSpec(
            num_scalar_prefetch=2,
            grid=(layers, -(-blocks // groups)),
            in_specs=[state_spec] * 3 + [grad_spec(place) for place in range(groups)],
            out_specs=[state_spec] * 3,
        ),
        cost_estimate=pl.CostEstimate(
            flops=20 * weights.size, bytes_accessed=26 * weights.size, transcendentals=weights.size
        ),
    )(group.reshape(1), scalars, weights, firsts, seconds, *([dealt] * groups))


def per_device(
    byte_tokens,
    seg_lengths,
    scripts,
    routes,
    step_count,
    attention_in,
    attention_out,
    feed_in,
    feed_out,
    embedding,
    norm_gains,
    first_attention_in,
    first_attention_out,
    first_feed_in,
    first_feed_out,
    first_embedding,
    first_norm_gains,
    second_attention_in,
    second_attention_out,
    second_feed_in,
    second_feed_out,
    second_embedding,
    second_norm_gains,
):
    groups = lax.axis_size("grp")
    members = lax.axis_size("dp")
    group = lax.axis_index("grp")
    member = lax.axis_index("dp")
    last = groups - 1
    is_decoder = group == last
    role = is_decoder.astype(jnp.int32)
    as_decoder = is_decoder.astype(FULL)
    decoder_slot = group ^ last
    micro, row_count = byte_tokens.shape[1:]
    tokens_here = micro * row_count
    shard_width = attention_in.shape[1]
    width = shard_width * members
    inner = attention_in.shape[2] // 3
    shard_inner = inner // members
    own_inner = inner // groups
    own_packed = 3 * own_inner
    own_width = width // groups
    shard_vocab = embedding.shape[0]
    vocab_size = shard_vocab * members
    capacity = 3 * row_count // (2 * members)
    slots = members * capacity
    deal = RowDeal(feed_out.shape[1], members, groups)
    scale_head = width ** (-0.5)

    tokens = byte_tokens[0]
    lengths = seg_lengths[0]
    bounds = jnp.cumsum(lengths, 1)
    position = jnp.arange(row_count, dtype=jnp.int32)
    segment = jnp.sum((position[None, :, None] >= bounds[:, None, :]).astype(jnp.int32), 2)
    same_row = segment[:, :, None] == segment[:, None, :]
    allowed_self = same_row & (
        jnp.logical_not(is_decoder) | (position[None, None, :] <= position[None, :, None])
    )
    starts = jnp.concatenate(
        [jnp.ones((micro, 1), bool), segment[:, 1:] != segment[:, :-1]], 1
    )
    previous = jnp.concatenate([jnp.zeros((micro, 1), jnp.int32), tokens[:, :-1]], 1)
    shifted = jnp.where(starts, 0, previous)
    inputs = jnp.where(is_decoder, shifted, tokens).reshape(tokens_here)
    target = routes[0, :, :, 0]
    hits = (target[:, :, None] == jnp.arange(members)[None, None, :]).astype(FULL)
    hits = hits * (1.0 - as_decoder)
    earlier = (position[:, None] > position[None, :]).astype(FULL)
    order = jnp.einsum("tu,bum->btm", earlier, hits, preferred_element_type=FULL)
    place = jnp.sum((order + capacity * jnp.arange(members, dtype=FULL)) * hits, 2)
    place = jnp.where(jnp.sum(hits, 2) > 0, place, -1.0)
    place = jnp.stack([place] + [send(place, step) for step in range(1, groups)])
    chosen = (
        place[..., None] == jnp.arange(slots, dtype=FULL)[None, None, None, :]
    ).astype(LOW)
    route_counts = jnp.sum(hits, 1)
    local_counts = (
        jnp.sum(
            jnp.where(scripts[0][..., None] == jnp.arange(3), lengths[..., None], 0), (0, 1)
        ).astype(FULL)
        * as_decoder
    )

    def pick(array):
        return lax.dynamic_index_in_dim(array, role, 0, keepdims=False).astype(LOW)

    def gather(value):
        return lax.all_gather(value, "dp", axis=0, tiled=True)

    def scatter(value):
        return lax.psum_scatter(value, "dp", scatter_dimension=0, tiled=True)

    extra = jnp.concatenate(
        [norm_gains.reshape(-1), local_counts, route_counts.reshape(-1)]
    ).astype(LOW)
    extra = jnp.pad(extra, (0, 8 * width - extra.shape[0])).reshape(8, width)
    packed_table = lax.all_gather(
        jnp.concatenate([embedding.astype(LOW), extra], 0), "dp", axis=0, tiled=False
    )
    table = packed_table[:, :shard_vocab].reshape(vocab_size, width)
    extras = packed_table[:, shard_vocab:].reshape(members, 8 * width)
    gain_size = 7 * shard_width
    gains = (
        extras[:, :gain_size].reshape(members, 7, shard_width).transpose(1, 0, 2).reshape(7, width)
    ).astype(FULL)
    counts = jnp.sum(extras[:, gain_size : gain_size + 3].astype(FULL), 0)
    scale_kind = 1.0 / (3.0 * jnp.maximum(counts, 1.0))
    came = extras[:, gain_size + 3 : gain_size + 3 + micro * members].astype(FULL)
    came = came.reshape(members, micro, members)
    came = lax.dynamic_index_in_dim(came, member, 2, keepdims=False)
    came = jnp.stack([came] + [send(came, step) for step in range(1, groups)])

    w_self_in = gather(pick(attention_in))

    onehot_inputs = (inputs[:, None] == jnp.arange(vocab_size)[None, :]).astype(LOW)
    stream0 = matmul(onehot_inputs, table)
    gain_self = jnp.where(is_decoder, gains[3], gains[0])
    normed_self = root_norm(stream0, gain_self).astype(LOW)
    packed_flat = matmul(normed_self, w_self_in).astype(LOW)
    w_self_out = gather(tie(pick(attention_out), table))
    dealt_in = deal_columns(tie(feed_in, table), group, groups)
    w_enc_in = gather(dealt_in[0])
    packed = packed_flat.reshape(micro, row_count, 3 * inner)
    q_self, k_self, v_self = (
        packed[:, :, :inner],
        packed[:, :, inner : 2 * inner],
        packed[:, :, 2 * inner :],
    )
    attended_self, shares_self = attend(q_self, k_self, v_self, allowed_self)
    attended_self = attended_self.reshape(tokens_here, inner)
    w_enc_out = deal.gather(tie(feed_out[0].astype(LOW), packed_flat), group, member)
    stream1 = stream0 + matmul(attended_self, w_self_out)

    gain_next = jnp.where(is_decoder, gains[4], gains[1])
    normed_next = root_norm(stream1, gain_next).astype(LOW)
    all_next = gather_groups(normed_next)
    cross_in = attention_in[2].reshape(shard_width, 3, groups, own_inner)
    own_cross = lax.dynamic_index_in_dim(cross_in, group, 2, keepdims=False)
    own_cross = own_cross.reshape(shard_width, own_packed).astype(LOW)
    w_cross = gather(tie(own_cross, normed_next))
    w_query, w_memory = w_cross[:, :own_inner], w_cross[:, own_inner:]
    w_cross_out = gather(tie(attention_out[2].astype(LOW), normed_next))
    w_dec_in = gather(tie(dealt_in[1], all_next))
    hidden_enc = matmul(all_next, w_enc_in)
    gated_enc = gate_apply(hidden_enc).astype(LOW)
    w_dec_out = deal.gather(tie(feed_out[1].astype(LOW), gated_enc), group, member)
    stream2e = stream1 + reduce_groups(matmul(gated_enc, w_enc_out))
    states = root_norm(stream2e, gains[2]).astype(LOW)
    all_states = gather_groups(states)
    memory_rows = matmul(all_states, w_memory).astype(LOW)

    def enter(slot):
        return slot + (slot >= decoder_slot).astype(jnp.int32)

    def enter_back(slot):
        return slot - (decoder_slot < slot).astype(jnp.int32)

    def reorder(array, places):
        return jnp.stack(
            [lax.dynamic_index_in_dim(array, index, 0, keepdims=False) for index in places]
        )

    encoder_slots = [enter(slot) for slot in range(last)]
    placed = jnp.einsum(
        "gbts,gbtd->gbsd",
        reorder(chosen, encoder_slots),
        reorder(memory_rows.reshape(groups, micro, row_count, 2 * own_inner), encoder_slots),
        preferred_element_type=FULL,
    ).astype(LOW)
    outgoing = placed.reshape(last, micro, members, capacity, 2 * own_inner)
    outgoing = outgoing.transpose(2, 1, 0, 3, 4)
    outgoing = outgoing.reshape(members, micro * last * capacity, 2 * own_inner)
    arrived = lax.all_to_all(outgoing, "dp", split_axis=0, concat_axis=0, tiled=True)
    key_count = members * last * capacity
    memory = arrived.reshape(members, micro, last * capacity, 2 * own_inner)
    memory = memory.transpose(1, 0, 2, 3).reshape(micro, key_count, 2 * own_inner)
    present = (
        jnp.arange(capacity, dtype=FULL)[None, None, None, :]
        < reorder(came, encoder_slots).transpose(2, 1, 0)[..., None]
    ).reshape(micro, key_count)
    allowed_cross = jnp.broadcast_to(present[:, None, :], (micro, row_count, key_count))

    cross_input = lax.dynamic_index_in_dim(
        all_next.reshape(groups, tokens_here, width), decoder_slot, 0, keepdims=False
    )
    queries = matmul(cross_input, w_query).astype(LOW).reshape(micro, row_count, own_inner)
    keys, values = memory[:, :, :own_inner], memory[:, :, own_inner:]
    attended_own, shares_cross = attend(queries, keys, values, allowed_cross)
    attended_own = attended_own.reshape(tokens_here, own_inner)
    attended_cross = jnp.concatenate(
        [send(attended_own, last ^ source, [source]) for source in range(last)] + [attended_own],
        1,
    )
    stream2d = stream1 + matmul(attended_cross, w_cross_out)

    all_dec = spread_last(root_norm(stream2d, gains[5]).astype(LOW), is_decoder)
    hidden_dec = matmul(all_dec, w_dec_in)
    gated_dec = gate_apply(hidden_dec).astype(LOW)
    stream3 = stream2d + collect_last(matmul(gated_dec, w_dec_out))

    head_in = (root_norm(stream3, gains[6]) * scale_head).astype(LOW)
    logits = transposed_right(head_in, table)
    row_max = jnp.max(logits, -1, keepdims=True)
    raised = jnp.exp(logits - row_max)
    row_total = jnp.sum(raised, -1, keepdims=True)
    flat_tokens = tokens.reshape(tokens_here)
    onehot_vocab = (jnp.arange(vocab_size)[None, :] == flat_tokens[:, None]).astype(FULL)
    log_total = row_max[:, 0] + jnp.log(row_total[:, 0])
    picked = jnp.sum(logits * onehot_vocab, 1)
    token_kind = jnp.sum(
        jnp.where(
            segment[:, :, None] == jnp.arange(lengths.shape[1])[None, None, :],
            scripts[0][:, None, :],
            0,
        ),
        2,
    ).reshape(tokens_here)
    weight = jnp.sum(
        jnp.where(token_kind[:, None] == jnp.arange(3)[None, :], scale_kind[None, :], 0.0), 1
    )
    weight = weight * as_decoder
    loss_part = jnp.sum((log_total - picked) * weight)
    grad_logits = ((raised / row_total - onehot_vocab) * weight[:, None]).astype(LOW)
    cotangent, gain_six = root_norm_back(
        stream3, gains[6], matmul(grad_logits, table) * scale_head
    )

    def feed_back(hidden, grad_all, w_in, w_out):
        unused, pull = jax.vjp(gate_apply, hidden)
        grad_hidden = pull(transposed_right(grad_all, w_out))[0].astype(LOW)
        return grad_hidden, transposed_right(grad_hidden, w_in)

    grad_all_dec = spread_last(cotangent.astype(LOW), is_decoder)
    grad_hidden_dec, part = feed_back(hidden_dec, grad_all_dec, w_dec_in, w_dec_out)
    grad_dec_in = transposed_left(all_dec, grad_hidden_dec).astype(LOW)
    grad_dec_out = deal.arrange(
        transposed_left(gated_dec, grad_all_dec).astype(LOW), group
    )
    collected, grad_dec_in, grad_dec_out = lax.optimization_barrier(
        (collect_last(part), grad_dec_in, grad_dec_out)
    )
    owned_dec_in = scatter(grad_dec_in)
    owned_dec_out = scatter(grad_dec_out)
    grad_stream, gain_five = root_norm_back(stream2d, gains[5], collected)
    cotangent = cotangent + grad_stream

    grad_low = cotangent.astype(LOW)
    grad_attended = transposed_right(grad_low, w_cross_out).astype(LOW)
    grad_own = jnp.where(is_decoder, grad_attended[:, last * own_inner :], 0)
    for source in range(last):
        grad_own = grad_own + send(
            grad_attended[:, source * own_inner : (source + 1) * own_inner], last ^ source, [last]
        )
    grad_q, grad_k, grad_v = attend_back(
        queries, keys, values, shares_cross, grad_own.reshape(micro, row_count, own_inner)
    )
    grad_memory = jnp.concatenate([grad_k, grad_v], 2)
    grad_memory = grad_memory.reshape(micro, members, last * capacity, 2 * own_inner)
    grad_memory = grad_memory.transpose(1, 0, 2, 3).reshape(outgoing.shape)
    reached = lax.all_to_all(grad_memory, "dp", split_axis=0, concat_axis=0, tiled=True)
    grad_q = grad_q.reshape(tokens_here, own_inner)
    grad_query_in = transposed_left(cross_input, grad_q)
    collected = collect_last(transposed_right(grad_q, w_query))
    grad_cross_out = transposed_left(attended_cross, grad_low).astype(LOW)
    grad_table = transposed_left(grad_logits, head_in)
    reached, grad_query_in, grad_cross_out, collected, grad_table = lax.optimization_barrier(
        (reached, grad_query_in, grad_cross_out, collected, grad_table)
    )
    owned_cross_out = scatter(grad_cross_out)
    reached = reached.reshape(members, micro, last, capacity, 2 * own_inner)
    reached = reached.transpose(2, 1, 0, 3, 4).reshape(last, micro, slots, 2 * own_inner)
    grad_rows = jnp.einsum(
        "gbts,gbsd->gbtd",
        chosen,
        reorder(reached, [jnp.minimum(enter_back(slot), last - 1) for slot in range(groups)]),
        preferred_element_type=FULL,
    )
    grad_rows = grad_rows.astype(LOW).reshape(groups * tokens_here, 2 * own_inner)
    grad_stream, gain_four = root_norm_back(stream1, gains[4], collected)
    cotangent_dec = cotangent + grad_stream

    reduced = reduce_groups(transposed_right(grad_rows, w_memory))
    grad_memory_in = transposed_left(all_states, grad_rows)
    reduced, grad_cross_in = lax.optimization_barrier(
        (reduced, jnp.concatenate([grad_query_in, grad_memory_in], 1))
    )
    owned_cross_in = scatter(grad_cross_in)
    cotangent_enc, gain_two = root_norm_back(stream2e, gains[2], reduced)
    grad_low = jnp.where(is_decoder, 0.0, cotangent_enc).astype(LOW)
    grad_all_enc = gather_groups(grad_low)
    grad_hidden_enc, part = feed_back(hidden_enc, grad_all_enc, w_enc_in, w_enc_out)
    grad_enc_in = transposed_left(all_next, grad_hidden_enc).astype(LOW)
    grad_enc_out = deal.arrange(
        transposed_left(gated_enc, grad_all_enc).astype(LOW), group
    )
    reduced, grad_enc_in, grad_enc_out = lax.optimization_barrier(
        (reduce_groups(part), grad_enc_in, grad_enc_out)
    )
    owned_enc_in = scatter(grad_enc_in)
    owned_enc_out = scatter(grad_enc_out)
    grad_stream, gain_one = root_norm_back(stream1, gains[1], reduced)
    cotangent_enc = cotangent_enc + grad_stream

    cotangent = jnp.where(is_decoder, cotangent_dec, cotangent_enc)
    grad_low = cotangent.astype(LOW)
    grad_attended = transposed_right(grad_low, w_self_out).astype(LOW)
    grads = attend_back(
        q_self, k_self, v_self, shares_self, grad_attended.reshape(micro, row_count, inner)
    )
    grad_packed = jnp.concatenate(grads, 2).reshape(tokens_here, 3 * inner)
    grad_stream, gain_zero = root_norm_back(
        stream0, gain_self, transposed_right(grad_packed, w_self_in)
    )
    cotangent = cotangent + grad_stream
    grad_lookup = lax.dot_general(
        onehot_inputs.astype(FULL),
        cotangent,
        (((0,), (0,)), ((), ())),
        precision=lax.Precision.HIGHEST,
        preferred_element_type=FULL,
    )
    grad_table = grad_table + grad_lookup

    all_normed, all_attended = (
        gather_groups(tie(normed_self, all_next)),
        gather_groups(tie(attended_self, all_next)),
    )

    def exchange_columns(value, columns):
        pieces = jnp.stack(
            [value[:, start : start + columns] for start in range(0, groups * columns, columns)]
        )
        mine = by_group(pieces, group)
        return jnp.concatenate(
            [mine[0]] + [send(mine[step], step) for step in range(1, groups)], 0
        )

    slot_of = (jnp.arange(groups * tokens_here) // tokens_here)[:, None]
    from_encoder = slot_of != decoder_slot

    def both_roles(left, right):
        right_slots = right.reshape(groups, tokens_here, -1)
        left_slots = left.reshape(groups, tokens_here, -1)
        return (
            transposed_left(left, jnp.where(from_encoder, right, 0)),
            transposed_left(
                lax.dynamic_index_in_dim(left_slots, decoder_slot, 0, keepdims=False),
                lax.dynamic_index_in_dim(right_slots, decoder_slot, 0, keepdims=False),
            ),
        )

    self_in_enc, self_in_dec = both_roles(all_normed, exchange_columns(grad_packed, own_packed))
    self_out_enc, self_out_dec = both_roles(all_attended, exchange_columns(grad_low, own_width))
    self_out = jnp.stack(
        [
            self_out_enc.reshape(members, shard_inner, own_width),
            self_out_dec.reshape(members, shard_inner, own_width),
        ],
        1,
    ).reshape(width, own_width)
    owned_self = scatter(jnp.concatenate([self_in_enc, self_in_dec, self_out], 1))

    encoder_only = 1.0 - as_decoder
    grad_gains = jnp.stack(
        [
            gain_zero * encoder_only,
            gain_one * encoder_only,
            gain_two * encoder_only,
            gain_zero * as_decoder,
            gain_four * as_decoder,
            gain_five * as_decoder,
            gain_six * as_decoder,
        ]
    )
    gain_rows = grad_gains.reshape(7, members, shard_width).transpose(1, 0, 2)
    gain_rows = gain_rows.reshape(members, gain_size)
    scalars = jnp.concatenate([loss_part[None], local_counts])
    gain_rows = jnp.concatenate(
        [gain_rows, jnp.broadcast_to(scalars[None], (members, 4))], 1
    )
    gain_rows = jnp.pad(gain_rows, ((0, 0), (0, 8 * width - gain_rows.shape[1])))
    last_pack = jnp.concatenate(
        [
            grad_table.reshape(members, shard_vocab, width),
            gain_rows.reshape(members, 8, width),
        ],
        1,
    )
    owned_pack = scatter(last_pack.reshape(members * (shard_vocab + 8), width))

    def every(value):
        return gather_groups(value).reshape((groups,) + value.shape)

    every_dec_in, every_dec_out = every(owned_dec_in), every(owned_dec_out)
    every_enc_in, every_enc_out = every(owned_enc_in), every(owned_enc_out)
    summed_pack = sum(by_group(every(owned_pack), group))
    grad_embedding = summed_pack[:shard_vocab]
    summed_rest = summed_pack[shard_vocab:].reshape(-1)
    grad_norm_gains = summed_rest[:gain_size].reshape(7, shard_width)
    loss_value = summed_rest[gain_size]
    total_counts = summed_rest[gain_size + 1 : gain_size + 4]
    cross_parts = by_group(every(owned_cross_in), group)
    self_parts = by_group(every(owned_self), group)
    final_cross_out = spread_last(owned_cross_out, is_decoder).astype(FULL)
    final_attention_in = jnp.stack(
        [
            jnp.concatenate([part[:, :own_packed] for part in self_parts], 1),
            jnp.concatenate([part[:, own_packed : 2 * own_packed] for part in self_parts], 1),
            jnp.concatenate(
                [
                    part[:, own_inner * kind : own_inner * (kind + 1)]
                    for kind in range(3)
                    for part in cross_parts
                ],
                1,
            ),
        ]
    )
    final_attention_out = jnp.stack(
        [
            jnp.concatenate([part[:shard_inner, 2 * own_packed :] for part in self_parts], 1),
            jnp.concatenate([part[shard_inner:, 2 * own_packed :] for part in self_parts], 1),
            final_cross_out,
        ]
    )
    final_feed_out = jnp.stack(
        [
            deal.restore(jnp.stack(by_group(parts, group)), member)
            for parts in (every_enc_out, every_dec_out)
        ]
    ).astype(FULL)

    def square(value):
        value = value.astype(FULL)
        return jnp.sum(value * value)

    first_group = (group == 0).astype(FULL)
    squares = (
        square(owned_enc_in)
        + square(owned_dec_in)
        + square(owned_enc_out)
        + square(owned_dec_out)
        + square(owned_cross_in)
        + square(owned_self)
        + as_decoder * square(owned_cross_out)
        + first_group * (square(grad_embedding) + square(grad_norm_gains))
    )
    norm = jnp.sqrt(lax.psum(squares, ("grp", "dp")))
    factor = jnp.minimum(1.0, CLIP / (norm + 1e-06))
    step_value = step_count[0].astype(FULL)
    fix_one = 1.0 - BETA_ONE**step_value
    fix_two = 1.0 - BETA_TWO**step_value
    new_feed_in = feed_in_step(
        feed_in,
        first_feed_in,
        second_feed_in,
        (every_enc_in, every_dec_in),
        jnp.stack([factor, fix_one, fix_two]),
        group,
    )

    def step(weight, first, second, gradient, decay):
        return adam(weight, first, second, gradient, factor, fix_one, fix_two, decay)

    results = [
        step(attention_in, first_attention_in, second_attention_in, final_attention_in, DECAY),
        step(attention_out, first_attention_out, second_attention_out, final_attention_out, DECAY),
        new_feed_in,
        step(feed_out, first_feed_out, second_feed_out, final_feed_out, DECAY),
        step(embedding, first_embedding, second_embedding, grad_embedding, DECAY),
        step(norm_gains, first_norm_gains, second_norm_gains, grad_norm_gains, 0.0),
    ]
    return (
        *(result[0] for result in results),
        *(result[1] for result in results),
        *(result[2] for result in results),
        loss_value,
        total_counts,
        norm,
    )


def solution(mesh):
    weights = (
        P(None, "dp", None),
        P(None, "dp", None),
        P(None, "dp", None),
        P(None, "dp", None),
        P("dp", None),
        P(None, "dp"),
    )
    in_specs = (
        P(("grp", "dp"), None, None),
        P(("grp", "dp"), None, None),
        P(("grp", "dp"), None, None),
        P(("grp", "dp"), None, None, None),
        P(),
    ) + 3 * weights
    out_specs = 3 * weights + (P(), P(), P())
    return jax.shard_map(
        per_device, mesh=mesh, in_specs=in_specs, out_specs=out_specs, check_vma=False
    )
```

time: 3500 us -> 1390 us (0.40)
  waiting for transfers between devices: 2300 us -> 497 us
  local copies, waits for them, and re-layouts: 509 us -> 176 us
  blocking collectives: 172 us -> 37 us
  starting transfers between devices: 13.6 us -> 136 us
  matrix products: 291 us -> 172 us
  other arithmetic: 171 us -> 275 us
  Pallas kernels: 0 us -> 57.5 us
    reduce_scatter x9 -> x8, waiting for transfers between devices: 1350 us -> 79.7 us  [scatter(): return lax.psum_scatter(value, 'dp', scatter_dimension=0, tiled=True)]
    psum x1 -> x0, waiting for transfers between devices: 447 us -> none  [per_device(): lax.psum((stacked_in, stacked_out, stacked_feed_in, stacked_feed_out, own...]
    another operation x20 -> x9, local copies, waits for them, and re-layouts: 307 us -> 7.89 us  [the longest x3 3.21 us: heads_of(): matrix.reshape(matrix.shape[0], matrix.shape[1], matrix.shape[2] // HEAD_...]
    all_gather x9, waiting for transfers between devices: 446 us -> 165 us  [the longest x6 91.1 us: gather(): return lax.all_gather(value, 'dp', axis=0, tiled=True)]
    ppermute x0 -> x102, waiting for transfers between devices: none -> 240 us  [send(): lax.ppermute(value, 'grp', [(source, source ^ step) for source in sources])]
    concatenate x0 -> x52, other arithmetic: none -> 140 us  [the longest x11 93.3 us: gather_groups(): jnp.concatenate([jnp.concatenate([left, left_one, left_more], 0), jnp.con...]
    ppermute x0 -> x102, starting transfers between devices: none -> 125 us  [send(): lax.ppermute(value, 'grp', [(source, source ^ step) for source in sources])]
    cond x65 -> x0, local copies, waits for them, and re-layouts: 111 us -> none  [the longest x5 109 us: run_role(): return lax.cond(active, worker, skipped, totals, *operands)]
  transfers between devices with their start and end apart: 23 -> 121, of which waited for: 18 -> 59; matrix products, arithmetic and copies ran while one was open for 12% -> 37% of each run, Pallas kernels for 0% -> 4%
where the time goes in v1:
time: 1390 us; the launch traced here: 1380 us
  waiting for transfers between devices  497 us (36%)
  other arithmetic  275 us (20%)
  local copies, waits for them, and re-layouts  176 us (13%)
  matrix products  172 us (12%)
  starting transfers between devices  136 us (10%)
  Pallas kernels  57.5 us (4%)
  blocking collectives  37 us (3%)
  between operations  26.5 us (2%)
    ppermute x102, waiting for transfers between devices, send(): lax.ppermute(value, 'grp', [(source, source ^ step) for source in sources])  240 us
    ppermute x102, starting transfers between devices, send(): lax.ppermute(value, 'grp', [(source, source ^ step) for source in sources])  125 us
    concatenate x11, other arithmetic, gather_groups(): jnp.concatenate([jnp.concatenate([left, left_one, left_more], 0), jnp.con...  93.3 us
    all_gather x6, waiting for transfers between devices, gather(): return lax.all_gather(value, 'dp', axis=0, tiled=True)  91.1 us
    reduce_scatter x8, waiting for transfers between devices, scatter(): return lax.psum_scatter(value, 'dp', scatter_dimension=0, tiled=True)  79.7 us
    all_gather x2, waiting for transfers between devices, gather(): held = lax.all_gather(piece, 'dp', axis=0, tiled=False)  52.6 us
    dot_general x12, matrix products, transposed_left(): lax.dot_general(left, right, (((0,), (0,)), ((), ())), preferred_element_...  47.6 us
    dot_general x10, matrix products, transposed_right(): lax.dot_general(left, right, (((1,), (1,)), ((), ())), preferred_element_...  47.1 us
  transfers between devices with their start and end apart: 121, of which 59 were waited for; matrix products, arithmetic and copies ran while one was open for 37% of the time, Pallas kernels for 4%

profile of v1, /device:TPU:0, one launch (start us, length us, event | category | flops | bytes accessed | tf_op | source)
XLA Modules:
  0.0 1376.6 jit_solution(2555701291252507429)
XLA Ops:
  19.1 21.2 %all-gather.23.cloned.1.call-done = bf16[448,1536]{1,0:T(8,128)(2,1)} async-done(((bf16[56,1536]{1,0:T(8,128)(2,1)}), bf16[448,1536]{1,0:T(8,128)(2,1)}) %all-gather.23.cloned.1.call-update) | async-done | bytes 1376272 | tf_op jit(solution)/shard_map/all_gather | solution.py:415
  42.7 17.3 %shard_map.382 = bf16[2,192,2048]{2,1,0:T(8,128)(2,1)} custom-call(s32[1]{0:T(128)} %bitcast.21.group_ref, f32[2,192,7936]{2,1,0:T(8,128)} %w_ref.1), custom_call_target="tpu_custom_call" | custom-call | tf_op jit(solution)/shard_map/pallas_call | solution.py:191
  73.9 39.2 %all-gather.25.cloned.1.call-done = bf16[1,1536,2304]{2,1,0:T(8,128)(2,1)} async-done(((bf16[1,192,2304]{2,1,0:T(8,128)(2,1)}), bf16[1,1536,2304]{2,1,0:T(8,128)(2,1)}) %all-gather.25.cloned.1.call-update) | async-done | bytes 7077904 | tf_op jit(solution)/shard_map/all_gather | solution.py:406
  125.2 20.3 %all-gather.15.cloned.1.call-done = bf16[768,1536]{1,0:T(8,128)(2,1)} async-done(((bf16[96,1536]{1,0:T(8,128)(2,1)}), bf16[768,1536]{1,0:T(8,128)(2,1)}) %all-gather.15.cloned.1.call-update) | async-done | bytes 2359312 | tf_op jit(solution)/shard_map/all_gather | solution.py:406
  164.1 15.0 %collective-permute-done.3 = bf16[512,768]{1,0:T(8,128)(2,1)S(1)} collective-permute-done((bf16[512,768]{1,0:T(8,128)(2,1)S(1)}, bf16[512,768]{1,0:T(8,128)(2,1)S(1)}, u32[]{:S(2)}, u32[]{:S(2)}) %collective-permute-start.3) | collective-permute-done | bytes 786464 | tf_op jit(solution)/shard_map/ppermute | solution.py:104
  180.0 31.6 %all-gather.27.cloned.1.call-done = bf16[1,1536,2048]{2,1,0:T(8,128)(2,1)} async-done(((bf16[1,192,2048]{2,1,0:T(8,128)(2,1)}), bf16[1,1536,2048]{2,1,0:T(8,128)(2,1)}) %all-gather.27.cloned.1.call-update) | async-done | bytes 6291472 | tf_op jit(solution)/shard_map/all_gather | solution.py:406
  211.5 9.8 fusion.10
  233.8 16.8 %all-gather.29.cloned.1.call-done = bf16[1024,1536]{1,0:T(8,128)(2,1)} async-done(((bf16[128,1536]{1,0:T(8,128)(2,1)}), bf16[1024,1536]{1,0:T(8,128)(2,1)}) %all-gather.29.cloned.1.call-update) | async-done | bytes 3145744 | tf_op jit(solution)/shard_map/all_gather | solution.py:227
  254.0 35.8 %all-gather.31.cloned.1.call-done = bf16[1024,1536]{1,0:T(8,128)(2,1)} async-done(((bf16[128,1536]{1,0:T(8,128)(2,1)}), bf16[1024,1536]{1,0:T(8,128)(2,1)}) %all-gather.31.cloned.1.call-update) | async-done | bytes 3145744 | tf_op jit(solution)/shard_map/all_gather | solution.py:227
  305.0 15.3 %collective-permute-done.11 = bf16[512,768]{1,0:T(8,128)(2,1)S(1)} collective-permute-done((bf16[512,768]{1,0:T(8,128)(2,1)S(1)}, bf16[512,768]{1,0:T(8,128)(2,1)S(1)}, u32[]{:S(2)}, u32[]{:S(2)}) %collective-permute-start.11) | collective-permute-done | bytes 786464 | tf_op jit(solution)/shard_map/ppermute | solution.py:104
  322.7 17.0 %maximum_maximum_fusion.1 = bf16[1024,1536]{1,0:T(8,128)(2,1)} fusion(bf16[256,768]{1,0:T(8,128)(2,1)S(1)} %copy-done.97, bf16[256,768]{1,0:T(8,128)(2,1)S(1)} %copy-done.89, bf16[256,768]{1,0:T(8,128)(2,1)S(1)} %copy-done.95, bf16[256,768]{1,0:T(8,128)(2,1)S(1)} %copy-done.43, bf16[512,768]{1,0:T(8,128)(2,1)} %collective-permute-done.1, ...), kind=kLoop, calls=%fused_computation.47 | loop fusion | flops 22020096 | bytes 6291456 | tf_op jit(solution)/shard_map/concatenate | solution.py:119
  374.3 11.4 collective-permute-done.10
  389.0 17.0 %maximum_maximum_fusion.2 = bf16[1024,1536]{1,0:T(8,128)(2,1)} fusion(bf16[256,768]{1,0:T(8,128)(2,1)S(1)} %get-tuple-element.248, bf16[256,768]{1,0:T(8,128)(2,1)S(1)} %copy-done.105, bf16[256,768]{1,0:T(8,128)(2,1)S(1)} %get-tuple-element.247, bf16[256,768]{1,0:T(8,128)(2,1)S(1)} %copy-done.50, bf16[512,768]{1,0:T(8,128)(2,1)} %collective-permute-done.16, ...), kind=kLoop, calls=%fused_computation.50 | loop fusion | flops 22020096 | bytes 6291456 | tf_op jit(solution)/shard_map/concatenate | solution.py:119
  473.2 20.5 %collective-permute-done.26 = bf16[256,768]{1,0:T(8,128)(2,1)S(1)} collective-permute-done((bf16[256,768]{1,0:T(8,128)(2,1)S(1)}, bf16[256,768]{1,0:T(8,128)(2,1)S(1)}, u32[]{:S(2)}, u32[]{:S(2)}) %collective-permute-start.26) | collective-permute-done | bytes 393248 | tf_op jit(solution)/shard_map/ppermute | solution.py:104
  538.3 17.9 %collective-permute-done.34 = bf16[256,768]{1,0:T(8,128)(2,1)S(1)} collective-permute-done((bf16[256,768]{1,0:T(8,128)(2,1)S(1)}, bf16[256,768]{1,0:T(8,128)(2,1)S(1)}, u32[]{:S(2)}, u32[]{:S(2)}) %collective-permute-start.34) | collective-permute-done | bytes 393248 | tf_op jit(solution)/shard_map/ppermute | solution.py:104
  556.4 9.2 collective-permute-done.36
  600.0 11.6 collective-permute-done.41
  685.7 18.7 %collective-permute-done.48 = bf16[512,768]{1,0:T(8,128)(2,1)S(1)} collective-permute-done((bf16[512,768]{1,0:T(8,128)(2,1)S(1)}, bf16[512,768]{1,0:T(8,128)(2,1)S(1)}, u32[]{:S(2)}, u32[]{:S(2)}) %collective-permute-start.48) | collective-permute-done | bytes 786464 | tf_op jit(solution)/shard_map/ppermute | solution.py:104
  704.8 9.5 collective-permute-done.49
  757.0 18.1 %fusion.58 = (f32[1024,1024]{1,0:T(8,128)S(1)}, f32[1024,1024]{1,0:T(8,128)S(1)}) fusion(f32[1024,2048]{1,0:T(8,128)} %copy-done.25, bf16[1024,1536]{1,0:T(8,128)(2,1)} %bitcast.379, bf16[256,768]{1,0:T(8,128)(2,1)S(1)} %get-tuple-element.237, bf16[256,768]{1,0:T(8,128)(2,1)} %copy-done.160, bf16[256,768]{1,0:T(8,128)(2,1)S(1)} %get-tuple-element.236, ...), kind=kOutput, calls=%fused_computation.151 | convolution fusion | flops 3266314240 | bytes 23068672 | tf_op jit(solution)/shard_map/dot_general | solution.py:34
  775.2 12.9 fusion.348
  792.6 18.7 %convolution_convert_fusion.1 = bf16[1536,2048]{1,0:T(8,128)(2,1)} fusion(f32[1024,1024]{1,0:T(8,128)} %copy-done.234, f32[1024,1024]{1,0:T(8,128)} %copy-done.233, bf16[256,768]{1,0:T(8,128)(2,1)S(1)} %copy-done.98, bf16[256,768]{1,0:T(8,128)(2,1)S(1)} %copy-done.90, bf16[256,768]{1,0:T(8,128)(2,1)S(1)} %copy-done.96, bf16[256,768]{1,0:T(8,128)(2,1)S(1)} %copy-done.44, ...), kind=kOutput, calls=%fused_computation.9 | convolution fusion | flops 6471811072 | bytes 17825792 | tf_op jit(solution)/shard_map/dot_general | solution.py:30
  919.3 16.9 %maximum_maximum_fusion.4 = bf16[1024,1536]{1,0:T(8,128)(2,1)} fusion(bf16[256,768]{1,0:T(8,128)(2,1)S(1)} %get-tuple-element.225, bf16[256,768]{1,0:T(8,128)(2,1)S(1)} %collective-permute-done.6, bf16[256,768]{1,0:T(8,128)(2,1)S(1)} %get-tuple-element.224, bf16[256,768]{1,0:T(8,128)(2,1)S(1)} %get-tuple-element.223, ...), kind=kLoop, calls=%fused_computation.54 | loop fusion | flops 22020096 | bytes 6291456 | tf_op jit(solution)/shard_map/concatenate | solution.py:119
  970.0 9.6 copy.323
  1086.3 17.3 %reduce-scatter.13.cloned.1.call-done = bf16[192,2048]{1,0:T(8,128)(2,1)} async-done(((bf16[1536,2048]{1,0:T(8,128)(2,1)}), bf16[192,2048]{1,0:T(8,128)(2,1)}) %reduce-scatter.13.cloned.1.call-update) | async-done | bytes 786448 | tf_op jit(solution)/shard_map/reduce_scatter | solution.py:409
  1119.4 16.2 %maximum_maximum_fusion.6 = bf16[768,2048]{1,0:T(8,128)(2,1)S(1)} fusion(bf16[192,1024]{1,0:T(8,128)(2,1)S(1)} %get-tuple-element.221, bf16[192,1024]{1,0:T(8,128)(2,1)S(1)} %copy-done.101, bf16[192,1024]{1,0:T(8,128)(2,1)S(1)} %get-tuple-element.220, bf16[192,1024]{1,0:T(8,128)(2,1)S(1)} %copy-done.46, bf16[384,1024]{1,0:T(8,128)(2,1)} %copy-done.143, ...), kind=kLoop, calls=%fused_computation.56 | loop fusion | flops 22020096 | bytes 6291456 | tf_op jit(solution)/shard_map/concatenate | solution.py:119
  1142.0 62.3 %reduce-scatter.25.cloned.1.call-done = f32[192,1536]{1,0:T(8,128)} async-done(((f32[1536,1536]{1,0:T(8,128)}), f32[192,1536]{1,0:T(8,128)}) %reduce-scatter.25.cloned.1.call-update) | async-done | bytes 1179664 | tf_op jit(solution)/shard_map/reduce_scatter | solution.py:409
  1208.4 17.6 %maximum_maximum_fusion.5 = bf16[768,2048]{1,0:T(8,128)(2,1)} fusion(bf16[192,1024]{1,0:T(8,128)(2,1)S(1)} %copy-done.115, bf16[192,1024]{1,0:T(8,128)(2,1)S(1)} %copy-done.111, bf16[192,1024]{1,0:T(8,128)(2,1)S(1)} %copy-done.114, bf16[192,1024]{1,0:T(8,128)(2,1)S(1)} %copy-done.54, bf16[384,1024]{1,0:T(8,128)(2,1)} %collective-permute-done.87, ...), kind=kLoop, calls=%fused_computation.55 | loop fusion | flops 22020096 | bytes 6291456 | tf_op jit(solution)/shard_map/concatenate | solution.py:119
  1238.6 37.0 %psum.7 = f32[]{:T(128)} all-reduce(f32[]{:T(128)S(6)} %add.619), channel_id=1, replica_groups=mesh['grp'=4,'dp'=8] {'grp','dp'}, use_global_device_ids=true, to_apply=%region_53.54 | all-reduce | flops 1 | bytes 8 | tf_op jit(solution)/shard_map/psum | solution.py:766
  1284.2 12.6 multiply_subtract_fusion
  1297.4 40.2 %shard_map.383 = (f32[2,192,7936]{2,1,0:T(8,128)}, f32[2,192,7936]{2,1,0:T(8,128)}, f32[2,192,7936]{2,1,0:T(8,128)}) custom-call(s32[1]{0:T(128)} %bitcast.21.group_ref, f32[3]{0:T(128)} %pad_maximum_fusion.50.scalar_ref, f32[2,192,7936]{2,1,0:T(8,128)} %w_ref.1, f32[2,192,7936]{2,1,0:T(8,128)} %m_ref.1, f32[2,192,7936]{2,1,0:T(8,128)} %v_ref.1, ...), custom_call_target="tpu_custom_call" | custom-call | flops 60948480 | bytes 79233024 | tf_op jit(solution)/shard_map/pallas_call | solution.py:303
  1354.0 11.4 multiply_subtract_fusion.1
  (1102 shorter events, 704.1 us)
Async XLA Ops:
  7.2 33.1 %all-gather.23.cloned.1.call-start = ((), (), s32[]{:S(2)}) async-start(), calls=%async_computation.20 | async-start | bytes 1548288 | tf_op jit(solution)/shard_map/all_gather | solution.py:415
  13.4 99.6 %all-gather.25.cloned.1.call-start = ((), (), s32[]{:S(2)}) async-start(), calls=%async_computation.21 | async-start | bytes 7962624 | tf_op jit(solution)/shard_map/all_gather | solution.py:406
  16.9 128.6 %all-gather.15.cloned.1.call-start = ((), (), s32[]{:S(2)}) async-start(), calls=%async_computation.10 | async-start | bytes 2654208 | tf_op jit(solution)/shard_map/all_gather | solution.py:406
  42.7 168.8 %all-gather.27.cloned.1.call-start = ((), (), s32[]{:S(2)}) async-start(), calls=%async_computation.22 | async-start | bytes 7077888 | tf_op jit(solution)/shard_map/all_gather | solution.py:406
  62.8 187.8 %all-gather.29.cloned.1.call-start = ((), (), s32[]{:S(2)}) async-start(), calls=%async_computation.23 | async-start | bytes 3538944 | tf_op jit(solution)/shard_map/all_gather | solution.py:227
  124.9 164.9 %all-gather.31.cloned.1.call-start = ((), (), s32[]{:S(2)}) async-start(), calls=%async_computation.24 | async-start | bytes 3538944 | tf_op jit(solution)/shard_map/all_gather | solution.py:227
  162.7 48.9 %collective-permute-start.1 = (bf16[512,768]{1,0:T(8,128)(2,1)}, bf16[512,768]{1,0:T(8,128)(2,1)}, u32[]{:S(2)}, u32[]{:S(2)}) collective-permute-start(bf16[512,768]{1,0:T(8,128)(2,1)} %pad_maximum_fusion.16), channel_id=1, source_target_pairs={{0,16},{8,24},{16,0},{24,8},{1,17},{9,25},{17,1},{25,9},{2,18},{10... | collective-permute-start | bytes 2359304 | tf_op jit(solution)/shard_map/ppermute | solution.py:104
  226.5 179.5 %all-gather.17.cloned.1.call-start = ((), (), s32[]{:S(2)}) async-start(), calls=%async_computation.11 | async-start | bytes 2211840 | tf_op jit(solution)/shard_map/all_gather | solution.py:406
  232.5 233.3 %all-gather.19.cloned.1.call-start = ((), (), s32[]{:S(2)}) async-start(), calls=%async_computation.12 | async-start | bytes 2654208 | tf_op jit(solution)/shard_map/all_gather | solution.py:406
  233.2 268.5 %all-gather.21.cloned.1.call-start = ((), (), s32[]{:S(2)}) async-start(), calls=%async_computation.13 | async-start | bytes 7077888 | tf_op jit(solution)/shard_map/all_gather | solution.py:406
  303.4 36.4 %collective-permute-start.13 = (bf16[512,768]{1,0:T(8,128)(2,1)}, bf16[512,768]{1,0:T(8,128)(2,1)}, u32[]{:S(2)}, u32[]{:S(2)}) collective-permute-start(bf16[512,768]{1,0:T(8,128)(2,1)} %pad_maximum_fusion.18), channel_id=1, source_target_pairs={{0,8},{8,0},{16,24},{24,16},{1,9},{9,1},{17,25},{25,17},{2,10},{10... | collective-permute-start | bytes 2359304 | tf_op jit(solution)/shard_map/ppermute | solution.py:104
  411.9 27.3 %all-to-all-start = ((bf16[8,144,384]{2,1,0:T(8,128)(2,1)}), bf16[8,144,384]{2,1,0:T(8,128)(2,1)}, u32[]{:S(2)}, u32[]{:S(2)}) async-start(bf16[8,144,384]{2,1,0:T(8,128)(2,1)} %bitcast.374), calls=%async_computation | async-start | bytes 1769472 | tf_op jit(solution)/shard_map/all_to_all | solution.py:491
  471.9 29.6 %collective-permute-start.28 = (bf16[256,768]{1,0:T(8,128)(2,1)S(1)}, bf16[256,768]{1,0:T(8,128)(2,1)S(1)}, u32[]{:S(2)}, u32[]{:S(2)}) collective-permute-start(bf16[256,768]{1,0:T(8,128)(2,1)S(1)} %broadcast_select_fusion.2), channel_id=1, source_target_pairs={{24,16},{8,0},{25,17},{9,1},{26,18},{10,2},{27,19},{11,3},{28,20},... | collective-permute-start | bytes 1179656 | tf_op jit(solution)/shard_map/ppermute | solution.py:104
  537.0 28.6 %collective-permute-start.36 = (bf16[256,768]{1,0:T(8,128)(2,1)S(1)}, bf16[256,768]{1,0:T(8,128)(2,1)S(1)}, u32[]{:S(2)}, u32[]{:S(2)}) collective-permute-start(bf16[256,768]{1,0:T(8,128)(2,1)S(1)} %broadcast_select_fusion), channel_id=1, source_target_pairs={{24,16},{8,0},{25,17},{9,1},{26,18},{10,2},{27,19},{11,3},{28,20},... | collective-permute-start | bytes 1179656 | tf_op jit(solution)/shard_map/ppermute | solution.py:104
  651.1 28.3 %all-to-all-start.1 = ((bf16[8,144,384]{2,1,0:T(8,128)(2,1)}), bf16[8,144,384]{2,1,0:T(8,128)(2,1)}, u32[]{:S(2)}, u32[]{:S(2)}) async-start(bf16[8,144,384]{2,1,0:T(8,128)(2,1)} %bitcast.375), calls=%async_computation.1 | async-start | bytes 1769472 | tf_op jit(solution)/shard_map/all_to_all | solution.py:578
  656.3 324.1 %reduce-scatter.21.cloned.1.call-start = ((), (), s32[]{:S(2)}) async-start(), calls=%async_computation.18 | async-start | bytes 2654208 | tf_op jit(solution)/shard_map/reduce_scatter | solution.py:409
  679.5 302.6 %reduce-scatter.19.cloned.1.call-start = ((), (), s32[]{:S(2)}) async-start(), calls=%async_computation.17 | async-start | bytes 3538944 | tf_op jit(solution)/shard_map/reduce_scatter | solution.py:409
  680.2 323.3 %reduce-scatter.27.cloned.1.call-start = ((), (), s32[]{:S(2)}) async-start(), calls=%async_computation.26 | async-start | bytes 4423680 | tf_op jit(solution)/shard_map/reduce_scatter | solution.py:409
  755.1 275.4 %reduce-scatter.23.cloned.1.call-start = ((), (), s32[]{:S(2)}) async-start(), calls=%async_computation.19 | async-start | bytes 3096576 | tf_op jit(solution)/shard_map/reduce_scatter | solution.py:409
  790.1 30.1 %collective-permute-start.58 = (bf16[512,768]{1,0:T(8,128)(2,1)}, bf16[512,768]{1,0:T(8,128)(2,1)}, u32[]{:S(2)}, u32[]{:S(2)}) collective-permute-start(bf16[512,768]{1,0:T(8,128)(2,1)} %pad_maximum_fusion.24), channel_id=1, source_target_pairs={{0,8},{8,0},{16,24},{24,16},{1,9},{9,1},{17,25},{25,17},{2,10},{10... | collective-permute-start | bytes 2359304 | tf_op jit(solution)/shard_map/ppermute | solution.py:104
  880.4 171.0 %reduce-scatter.17.cloned.1.call-start = ((), (), s32[]{:S(2)}) async-start(), calls=%async_computation.16 | async-start | bytes 3538944 | tf_op jit(solution)/shard_map/reduce_scatter | solution.py:409
  881.0 183.1 %reduce-scatter.15.cloned.1.call-start = ((), (), s32[]{:S(2)}) async-start(), calls=%async_computation.15 | async-start | bytes 7077888 | tf_op jit(solution)/shard_map/reduce_scatter | solution.py:409
  881.6 222.0 %reduce-scatter.13.cloned.1.call-start = ((), (), s32[]{:S(2)}) async-start(), calls=%async_computation.14 | async-start | bytes 7077888 | tf_op jit(solution)/shard_map/reduce_scatter | solution.py:409
  882.2 322.2 %reduce-scatter.25.cloned.1.call-start = ((), (), s32[]{:S(2)}) async-start(), calls=%async_computation.25 | async-start | bytes 10616832 | tf_op jit(solution)/shard_map/reduce_scatter | solution.py:409
  1080.3 30.2 %collective-permute-start.93 = (bf16[384,1024]{1,0:T(8,128)(2,1)}, bf16[384,1024]{1,0:T(8,128)(2,1)}, u32[]{:S(2)}, u32[]{:S(2)}) collective-permute-start(bf16[384,1024]{1,0:T(8,128)(2,1)} %pad_maximum_fusion.32), channel_id=1, source_target_pairs={{0,8},{8,0},{16,24},{24,16},{1,9},{9,1},{17,25},{25,17},{2,10},{10... | collective-permute-start | bytes 2359304 | tf_op jit(solution)/shard_map/ppermute | solution.py:104
  1085.5 33.0 %collective-permute-start.91 = (bf16[384,1024]{1,0:T(8,128)(2,1)}, bf16[384,1024]{1,0:T(8,128)(2,1)S(1)}, u32[]{:S(2)}, u32[]{:S(2)}) collective-permute-start(bf16[384,1024]{1,0:T(8,128)(2,1)} %pad_maximum_fusion.31), channel_id=1, source_target_pairs={{0,16},{8,24},{16,0},{24,8},{1,17},{9,25},{17,1},{25,9},{2,18},{10... | collective-permute-start | bytes 2359304 | tf_op jit(solution)/shard_map/ppermute | solution.py:104
  1114.5 25.4 %collective-permute-start.89 = (bf16[384,1024]{1,0:T(8,128)(2,1)}, bf16[384,1024]{1,0:T(8,128)(2,1)}, u32[]{:S(2)}, u32[]{:S(2)}) collective-permute-start(bf16[384,1024]{1,0:T(8,128)(2,1)} %pad_maximum_fusion.30), channel_id=1, source_target_pairs={{0,8},{8,0},{16,24},{24,16},{1,9},{9,1},{17,25},{25,17},{2,10},{10... | collective-permute-start | bytes 2359304 | tf_op jit(solution)/shard_map/ppermute | solution.py:104
  1117.1 91.3 %collective-permute-start.87 = (bf16[384,1024]{1,0:T(8,128)(2,1)}, bf16[384,1024]{1,0:T(8,128)(2,1)}, u32[]{:S(2)}, u32[]{:S(2)}) collective-permute-start(bf16[384,1024]{1,0:T(8,128)(2,1)} %pad_maximum_fusion.29), channel_id=1, source_target_pairs={{0,16},{8,24},{16,0},{24,8},{1,17},{9,25},{17,1},{25,9},{2,18},{10... | collective-permute-start | bytes 2359304 | tf_op jit(solution)/shard_map/ppermute | solution.py:104
  1206.9 69.5 %collective-permute-start.72 = (f32[192,768]{1,0:T(8,128)}, f32[192,768]{1,0:T(8,128)}, u32[]{:S(2)}, u32[]{:S(2)}) collective-permute-start(f32[192,768]{1,0:T(8,128)} %get-tuple-element.198), channel_id=1, source_target_pairs={{0,16},{8,24},{16,0},{24,8},{1,17},{9,25},{17,1},{25,9},{2,18},{10... | collective-permute-start | bytes 1769480 | tf_op jit(solution)/shard_map/ppermute | solution.py:104
  1226.0 55.1 %collective-permute-start.70 = (f32[192,768]{1,0:T(8,128)}, f32[192,768]{1,0:T(8,128)}, u32[]{:S(2)}, u32[]{:S(2)}) collective-permute-start(f32[192,768]{1,0:T(8,128)} %get-tuple-element.197), channel_id=1, source_target_pairs={{0,8},{8,0},{16,24},{24,16},{1,9},{9,1},{17,25},{25,17},{2,10},{10... | collective-permute-start | bytes 1769480 | tf_op jit(solution)/shard_map/ppermute | solution.py:104
  1278.8 62.1 %collective-permute-start.73 = (f32[384,768]{1,0:T(8,128)}, f32[384,768]{1,0:T(8,128)S(1)}, u32[]{:S(2)}, u32[]{:S(2)}) collective-permute-start(f32[384,768]{1,0:T(8,128)} %pad_maximum_fusion.15), channel_id=1, source_target_pairs={{0,8},{8,0},{16,24},{24,16},{1,9},{9,1},{17,25},{25,17},{2,10},{10... | collective-permute-start | bytes 3538952 | tf_op jit(solution)/shard_map/ppermute | solution.py:104
  1283.4 57.6 %collective-permute-start.71 = (f32[384,768]{1,0:T(8,128)}, f32[384,768]{1,0:T(8,128)S(1)}, u32[]{:S(2)}, u32[]{:S(2)}) collective-permute-start(f32[384,768]{1,0:T(8,128)} %pad_maximum_fusion.14), channel_id=1, source_target_pairs={{0,16},{8,24},{16,0},{24,8},{1,17},{9,25},{17,1},{25,9},{2,18},{10... | collective-permute-start | bytes 3538952 | tf_op jit(solution)/shard_map/ppermute | solution.py:104
  (328 other events, 3392.4 us)
Sparse Core Ops, SparseCore 0:
  13.6 26.6 all-gather.22
  42.5 70.5 all-gather.24
  115.3 30.1 all-gather.14
  147.6 63.8 all-gather.26
  213.6 36.9 all-gather.28
  252.6 37.1 all-gather.30
  292.0 26.8 all-gather.16
  321.1 31.1 all-gather.18
  354.5 63.8 all-gather.20
  679.6 33.4 reduce-scatter.20
  716.0 39.4 reduce-scatter.18
  758.2 46.6 reduce-scatter.26
  880.5 38.5 reduce-scatter.22
  922.0 39.3 reduce-scatter.16
  963.6 68.8 reduce-scatter.14
  1035.4 68.1 reduce-scatter.12
  1106.4 97.8 reduce-scatter.24

commit v2 on v1

--- a/solution.py
+++ b/solution.py
@@ -90,8 +90,8 @@
     gradient = gradient * factor
     first_moment = BETA_ONE * first_moment + (1.0 - BETA_ONE) * gradient
     second = BETA_TWO * second + (1.0 - BETA_TWO) * gradient * gradient
-    fixed_first = first_moment / fix_one
-    fixed_second = second / fix_two
+    fixed_first = first_moment * fix_one
+    fixed_second = second * fix_two
     weight = weight - LEARN_RATE * (
         fixed_first / (jnp.sqrt(fixed_second) + ADAM_EPS) + decay * weight
     )
@@ -109,20 +109,31 @@
     return value[:, :middle], value[:, middle:]
 
 
+def assemble_kernel(value_ref, one_ref, left_ref, two_ref, right_ref, out_ref):
+    rows, width = value_ref.shape
+    middle = width // 2
+    out_ref[:rows, :] = value_ref[...]
+    out_ref[rows : 2 * rows, :middle] = one_ref[...]
+    out_ref[2 * rows :, :middle] = left_ref[...]
+    out_ref[rows : 2 * rows, middle:] = right_ref[:rows, :]
+    out_ref[2 * rows : 3 * rows, middle:] = two_ref[...]
+    out_ref[3 * rows :, middle:] = right_ref[rows:, :]
+
+
 def gather_groups(value):
-    rows = value.shape[0]
+    rows, width = value.shape
     left, right = halves(value)
     left_one = send(left, 1)
     right_two = send(right, 2)
     left_more = send(jnp.concatenate([left, left_one], 0), 2)
     right_more = send(jnp.concatenate([right, right_two], 0), 1)
-    return jnp.concatenate(
-        [
-            jnp.concatenate([left, left_one, left_more], 0),
-            jnp.concatenate([right, right_more[:rows], right_two, right_more[rows:]], 0),
-        ],
-        1,
-    )
+    return pl.pallas_call(
+        assemble_kernel,
+        out_shape=jax.ShapeDtypeStruct((4 * rows, width), value.dtype),
+        cost_estimate=pl.CostEstimate(
+            flops=0, bytes_accessed=8 * rows * width * value.dtype.itemsize, transcendentals=0
+        ),
+    )(value, left_one, left_more, right_two, right_more)
 
 
 def reduce_groups(parts):
@@ -173,95 +184,96 @@
     return lax.optimization_barrier((value,) + others)[0]
 
 
-def deal_columns(feed_in, group, groups):
-    layers, rows, width = feed_in.shape
-    half = width // 2
-    blocks = half // LANES
-    own = -(-blocks // groups)
-
-    def kernel(group_ref, source_ref, out_ref):
-        place = pl.program_id(1) % own
-        inside = groups * place + group_ref[0] < blocks
-        out_ref[...] = jnp.where(inside, source_ref[...], 0.0).astype(LOW)
-
-    def source_map(layer, step, group_ref):
-        block = jnp.minimum(groups * (step % own) + group_ref[0], blocks - 1)
-        return (layer, 0, (step // own) * blocks + block)
-
-    return pl.pallas_call(
-        kernel,
-        out_shape=jax.ShapeDtypeStruct((layers, rows, 2 * own * LANES), LOW),
-        grid_spec=pltpu.PrefetchScalarGridSpec(
-            num_scalar_prefetch=1,
-            grid=(layers, 2 * own),
-            in_specs=[pl.BlockSpec((1, rows, LANES), source_map)],
-            out_specs=pl.BlockSpec((1, rows, LANES), lambda layer, step, ref: (layer, 0, step)),
-        ),
-    )(group.reshape(1), feed_in)
-
-
-class RowDeal:
-    def __init__(self, shard_rows, members, groups):
+class Deal:
+    def __init__(self, shard_rows, members, groups, group, member):
         self.rows = shard_rows
         self.members = members
         self.groups = groups
+        self.group = group
+        self.member = member
         self.round = groups * LANES
-        self.gap = self.round - shard_rows
         self.blocks = shard_rows * members // LANES
         self.own = -(-self.blocks // groups)
-        self.snug = self.gap > 0 and self.gap * members == LANES and self.own == members
-
-    def gather(self, shard, group, member):
+        gap = self.round - shard_rows
+        self.snug = gap > 0 and gap * members == LANES and self.own == members
+        self.gap = gap if self.snug else 0
+
+    def limit(self, block):
+        return LANES - self.gap - self.gap * block
+
+    def columns(self, feed_in):
+        layers, rows, width = feed_in.shape
+        groups, own, blocks = self.groups, self.own, self.blocks
+
+        def kernel(group_ref, source_ref, before_ref, out_ref):
+            place = pl.program_id(1) % own
+            group = group_ref[0]
+            lane = lax.broadcasted_iota(jnp.int32, out_ref.shape, 2)
+            whole = jnp.logical_or(group != groups - 1, self.gap == 0)
+            limit = jnp.where(whole, LANES, self.limit(place))
+            limit = jnp.where(groups * place + group < blocks, limit, jnp.minimum(limit, 0))
+            after = jnp.where(whole, LANES, self.limit(place) + self.gap)
+            after = jnp.where(place > 0, after, LANES)
+            kept = jnp.where(lane < limit, source_ref[...], 0.0)
+            out_ref[...] = jnp.where(lane >= after, before_ref[...], kept).astype(LOW)
+
+        def source_map(back):
+            def index(layer, step, group_ref):
+                block = groups * (step % own - back) + group_ref[0]
+                block = jnp.clip(block, 0, blocks - 1)
+                return (layer, 0, (step // own) * blocks + block)
+
+            return index
+
+        return pl.pallas_call(
+            kernel,
+            out_shape=jax.ShapeDtypeStruct((layers, rows, 2 * own * LANES), LOW),
+            grid_spec=pltpu.PrefetchScalarGridSpec(
+                num_scalar_prefetch=1,
+                grid=(layers, 2 * own),
+                in_specs=[
+                    pl.BlockSpec((1, rows, LANES), source_map(0)),
+                    pl.BlockSpec((1, rows, LANES), source_map(1)),
+                ],
+                out_specs=pl.BlockSpec((1, rows, LANES), lambda layer, step, ref: (layer, 0, step)),
+            ),
+        )(self.group.reshape(1), feed_in, feed_in)
+
+    def gather(self, shard):
         width = shard.shape[1]
         if not self.snug:
             whole = lax.all_gather(shard, "dp", axis=0, tiled=True)
             padded = jnp.pad(whole, ((0, self.own * self.round - whole.shape[0]), (0, 0)))
             dealt = padded.reshape(self.own, self.groups, LANES, width)
-            picked = lax.dynamic_index_in_dim(dealt, group, 1, keepdims=False)
+            picked = lax.dynamic_index_in_dim(dealt, self.group, 1, keepdims=False)
             return picked.reshape(self.own * LANES, width)
         padded = jnp.pad(shard, ((0, self.gap), (0, 0)))
         doubled = jnp.concatenate([padded, padded], 0)
-        piece = lax.dynamic_slice(
-            doubled, (self.gap * member + LANES * group, 0), (LANES, width)
+        start = self.gap * self.member + LANES * self.group
+        piece = lax.dynamic_slice(doubled, (start, 0), (LANES, width))
+        return lax.all_gather(piece, "dp", axis=0, tiled=True)
+
+    def arrange(self, grad):
+        if self.snug:
+            return grad
+        width = grad.shape[1]
+        spread = jnp.zeros((self.own, self.groups, LANES, width), grad.dtype)
+        spread = lax.dynamic_update_index_in_dim(
+            spread, grad.reshape(self.own, 1, LANES, width), self.group, 1
         )
-        held = lax.all_gather(piece, "dp", axis=0, tiled=False)
-        after = jnp.concatenate([held[1:], jnp.zeros_like(held[:1])], 0)
-        limit = (LANES - self.gap) - self.gap * jnp.arange(self.members)[:, None, None]
-        place = jnp.arange(LANES)[None, :, None]
-        wrapped = jnp.where(place < limit, held, after)
-        return jnp.where(group == self.groups - 1, wrapped, held).reshape(-1, width)
-
-    def arrange(self, grad, group):
-        width = grad.shape[1]
-        if not self.snug:
-            spread = jnp.zeros((self.own, self.groups, LANES, width), grad.dtype)
-            spread = lax.dynamic_update_index_in_dim(
-                spread, grad.reshape(self.own, 1, LANES, width), group, 1
-            )
-            return spread.reshape(-1, width)[: self.rows * self.members]
-        held = grad.reshape(self.members, LANES, width)
-        before = jnp.concatenate([jnp.zeros_like(held[:1]), held[:-1]], 0)
-        index = self.gap * jnp.arange(self.members)[:, None, None]
-        place = jnp.arange(LANES)[None, :, None]
-        wrapped = jnp.where(
-            place < (LANES - self.gap) - index,
-            held,
-            jnp.where(place >= LANES - index, before, jnp.zeros_like(held)),
-        )
-        held = jnp.where(group == self.groups - 1, wrapped, held)
-        return held.reshape(-1, width)
-
-    def restore(self, parts, member):
+        return spread.reshape(-1, width)[: self.rows * self.members]
+
+    def restore(self, parts):
         if not self.snug:
             return jnp.sum(parts, 0)
         width = parts.shape[2]
         line = parts.reshape(self.round, width)
         doubled = jnp.concatenate([line, line], 0)
-        start = (self.round - self.gap * member) % self.round
+        start = (self.round - self.gap * self.member) % self.round
         return lax.dynamic_slice(doubled, (start, 0), (self.rows, width))
 
 
-def feed_in_step(weights, firsts, seconds, dealt, scalars, group):
+def feed_in_step(weights, firsts, seconds, dealt, scalars, deal):
     layers, rows, width = weights.shape
     groups = dealt[0].shape[0]
     blocks = width // LANES
@@ -269,11 +281,23 @@
     own = dealt[0].shape[2] // (2 * LANES)
     dealt = jnp.stack(dealt)
 
+    def whence(place, step):
+        block = jnp.minimum(step * groups + place, blocks - 1)
+        block = block - (block >= half_blocks).astype(jnp.int32) * half_blocks
+        return block % groups, block // groups
+
     def kernel(group_ref, scalar_ref, w_ref, m_ref, v_ref, *rest):
-        grads, outs = rest[:groups], rest[groups:]
+        grads, outs = rest[: 2 * groups], rest[2 * groups :]
+        lane = lax.broadcasted_iota(jnp.int32, (rows, LANES), 1)
         for place in range(groups):
             lanes = slice(place * LANES, (place + 1) * LANES)
             gradient = grads[place][0, 0].astype(FULL)
+            if deal.gap:
+                source, index = whence(place, pl.program_id(1))
+                own_lanes = jnp.where(source == groups - 1, deal.limit(index), LANES)
+                gradient = jnp.where(
+                    lane < own_lanes, gradient, grads[groups + place][0, 0].astype(FULL)
+                )
             new = adam(
                 w_ref[0, :, lanes],
                 m_ref[0, :, lanes],
@@ -287,13 +311,14 @@
             for out, value in zip(outs, new):
                 out[0, :, lanes] = value
 
-    def grad_spec(place):
+    def grad_spec(place, further):
         def index(layer, step, group_ref, scalar_ref):
-            block = jnp.minimum(step * groups + place, blocks - 1)
-            part = (block >= half_blocks).astype(jnp.int32)
-            block = block - part * half_blocks
-            slot = jnp.bitwise_xor(group_ref[0], block % groups)
-            return (layer, slot, 0, part * own + block // groups)
+            source, index = whence(place, step)
+            part = (jnp.minimum(step * groups + place, blocks - 1) >= half_blocks).astype(jnp.int32)
+            slot = jnp.bitwise_xor(group_ref[0], source)
+            if further:
+                index = jnp.where(source == groups - 1, jnp.minimum(index + 1, own - 1), 0)
+            return (layer, slot, 0, part * own + index)
 
         return pl.BlockSpec((1, 1, rows, LANES), index)
 
@@ -306,13 +331,15 @@
         grid_spec=pltpu.PrefetchScalarGridSpec(
             num_scalar_prefetch=2,
             grid=(layers, -(-blocks // groups)),
-            in_specs=[state_spec] * 3 + [grad_spec(place) for place in range(groups)],
+            in_specs=[state_spec] * 3
+            + [grad_spec(place, False) for place in range(groups)]
+            + [grad_spec(place, True) for place in range(groups)],
             out_specs=[state_spec] * 3,
         ),
         cost_estimate=pl.CostEstimate(
             flops=20 * weights.size, bytes_accessed=26 * weights.size, transcendentals=weights.size
         ),
-    )(group.reshape(1), scalars, weights, firsts, seconds, *([dealt] * groups))
+    )(deal.group.reshape(1), scalars, weights, firsts, seconds, *([dealt] * (2 * groups)))
 
 
 def per_device(
@@ -362,7 +389,7 @@
     vocab_size = shard_vocab * members
     capacity = 3 * row_count // (2 * members)
     slots = members * capacity
-    deal = RowDeal(feed_out.shape[1], members, groups)
+    deal = Deal(feed_out.shape[1], members, groups, group, member)
     scale_head = width ** (-0.5)
 
     tokens = byte_tokens[0]
@@ -436,7 +463,7 @@
     normed_self = root_norm(stream0, gain_self).astype(LOW)
     packed_flat = matmul(normed_self, w_self_in).astype(LOW)
     w_self_out = gather(tie(pick(attention_out), table))
-    dealt_in = deal_columns(tie(feed_in, table), group, groups)
+    dealt_in = deal.columns(tie(feed_in, table))
     w_enc_in = gather(dealt_in[0])
     packed = packed_flat.reshape(micro, row_count, 3 * inner)
     q_self, k_self, v_self = (
@@ -446,7 +473,7 @@
     )
     attended_self, shares_self = attend(q_self, k_self, v_self, allowed_self)
     attended_self = attended_self.reshape(tokens_here, inner)
-    w_enc_out = deal.gather(tie(feed_out[0].astype(LOW), packed_flat), group, member)
+    w_enc_out = deal.gather(tie(feed_out[0].astype(LOW), packed_flat))
     stream1 = stream0 + matmul(attended_self, w_self_out)
 
     gain_next = jnp.where(is_decoder, gains[4], gains[1])
@@ -461,7 +488,7 @@
     w_dec_in = gather(tie(dealt_in[1], all_next))
     hidden_enc = matmul(all_next, w_enc_in)
     gated_enc = gate_apply(hidden_enc).astype(LOW)
-    w_dec_out = deal.gather(tie(feed_out[1].astype(LOW), gated_enc), group, member)
+    w_dec_out = deal.gather(tie(feed_out[1].astype(LOW), gated_enc))
     stream2e = stream1 + reduce_groups(matmul(gated_enc, w_enc_out))
     states = root_norm(stream2e, gains[2]).astype(LOW)
     all_states = gather_groups(states)
@@ -551,9 +578,7 @@
     grad_all_dec = spread_last(cotangent.astype(LOW), is_decoder)
     grad_hidden_dec, part = feed_back(hidden_dec, grad_all_dec, w_dec_in, w_dec_out)
     grad_dec_in = transposed_left(all_dec, grad_hidden_dec).astype(LOW)
-    grad_dec_out = deal.arrange(
-        transposed_left(gated_dec, grad_all_dec).astype(LOW), group
-    )
+    grad_dec_out = deal.arrange(transposed_left(gated_dec, grad_all_dec).astype(LOW))
     collected, grad_dec_in, grad_dec_out = lax.optimization_barrier(
         (collect_last(part), grad_dec_in, grad_dec_out)
     )
@@ -599,8 +624,13 @@
 
     reduced = reduce_groups(transposed_right(grad_rows, w_memory))
     grad_memory_in = transposed_left(all_states, grad_rows)
-    reduced, grad_cross_in = lax.optimization_barrier(
-        (reduced, jnp.concatenate([grad_query_in, grad_memory_in], 1))
+    reduced, grad_cross_in, owned_dec_in, owned_dec_out = lax.optimization_barrier(
+        (
+            reduced,
+            jnp.concatenate([grad_query_in, grad_memory_in], 1),
+            owned_dec_in,
+            owned_dec_out,
+        )
     )
     owned_cross_in = scatter(grad_cross_in)
     cotangent_enc, gain_two = root_norm_back(stream2e, gains[2], reduced)
@@ -608,11 +638,11 @@
     grad_all_enc = gather_groups(grad_low)
     grad_hidden_enc, part = feed_back(hidden_enc, grad_all_enc, w_enc_in, w_enc_out)
     grad_enc_in = transposed_left(all_next, grad_hidden_enc).astype(LOW)
-    grad_enc_out = deal.arrange(
-        transposed_left(gated_enc, grad_all_enc).astype(LOW), group
-    )
-    reduced, grad_enc_in, grad_enc_out = lax.optimization_barrier(
-        (reduce_groups(part), grad_enc_in, grad_enc_out)
+    grad_enc_out = deal.arrange(transposed_left(gated_enc, grad_all_enc).astype(LOW))
+    reduced, grad_enc_in, grad_enc_out, owned_cross_in, owned_cross_out = (
+        lax.optimization_barrier(
+            (reduce_groups(part), grad_enc_in, grad_enc_out, owned_cross_in, owned_cross_out)
+        )
     )
     owned_enc_in = scatter(grad_enc_in)
     owned_enc_out = scatter(grad_enc_out)
@@ -676,7 +706,9 @@
         ],
         1,
     ).reshape(width, own_width)
-    owned_self = scatter(jnp.concatenate([self_in_enc, self_in_dec, self_out], 1))
+    owned_self = scatter(
+        tie(jnp.concatenate([self_in_enc, self_in_dec, self_out], 1), owned_enc_in, owned_enc_out)
+    )
 
     encoder_only = 1.0 - as_decoder
     grad_gains = jnp.stack(
@@ -704,7 +736,7 @@
         ],
         1,
     )
-    owned_pack = scatter(last_pack.reshape(members * (shard_vocab + 8), width))
+    owned_pack = scatter(tie(last_pack.reshape(members * (shard_vocab + 8), width), owned_self))
 
     def every(value):
         return gather_groups(value).reshape((groups,) + value.shape)
@@ -743,7 +775,7 @@
     )
     final_feed_out = jnp.stack(
         [
-            deal.restore(jnp.stack(by_group(parts, group)), member)
+            deal.restore(jnp.stack(by_group(parts, group)))
             for parts in (every_enc_out, every_dec_out)
         ]
     ).astype(FULL)
@@ -763,18 +795,26 @@
         + as_decoder * square(owned_cross_out)
         + first_group * (square(grad_embedding) + square(grad_norm_gains))
     )
-    norm = jnp.sqrt(lax.psum(squares, ("grp", "dp")))
+    squares = squares.reshape(1)
+    for step in (1, 2):
+        squares = squares + send(squares, step)
+    step = 1
+    while step < members:
+        pairs = [(source, source ^ step) for source in range(members)]
+        squares = squares + lax.ppermute(squares, "dp", pairs)
+        step *= 2
+    norm = jnp.sqrt(squares[0])
     factor = jnp.minimum(1.0, CLIP / (norm + 1e-06))
     step_value = step_count[0].astype(FULL)
-    fix_one = 1.0 - BETA_ONE**step_value
-    fix_two = 1.0 - BETA_TWO**step_value
+    fix_one = 1.0 / (1.0 - BETA_ONE**step_value)
+    fix_two = 1.0 / (1.0 - BETA_TWO**step_value)
     new_feed_in = feed_in_step(
         feed_in,
         first_feed_in,
         second_feed_in,
         (every_enc_in, every_dec_in),
         jnp.stack([factor, fix_one, fix_two]),
-        group,
+        deal,
     )
 
     def step(weight, first, second, gradient, decay):

time: 1390 us -> 1270 us (0.914)
  other arithmetic: 275 us -> 161 us
  Pallas kernels: 57.5 us -> 99.1 us
  blocking collectives: 37 us -> 0 us
  local copies, waits for them, and re-layouts: 176 us -> 143 us
  starting transfers between devices: 136 us -> 154 us
    concatenate x12 -> x0, other arithmetic: 101 us -> none  [the longest x11 93.3 us: gather_groups(): jnp.concatenate([jnp.concatenate([left, left_one, left_more], 0), jnp.con...]
    reduce_scatter x8, waiting for transfers between devices: 79.7 us -> 1.76 us  [scatter(): return lax.psum_scatter(value, 'dp', scatter_dimension=0, tiled=True)]
    ppermute x102 -> x104, waiting for transfers between devices: 240 us -> 317 us  [send(): lax.ppermute(value, 'grp', [(source, source ^ step) for source in sources])]
    pallas_call x1 -> x13, Pallas kernels: 17.3 us -> 59.5 us  [the longest x12 41.3 us: gather_groups(): pl.pallas_call(assemble_kernel, out_shape=jax.ShapeDtypeStruct((4 * rows,...]
    psum x1 -> x0, blocking collectives: 37 us -> none  [per_device(): norm = jnp.sqrt(lax.psum(squares, ('grp', 'dp')))]
    all_to_all x1, waiting for transfers between devices: 2.73 us -> 34.9 us  [per_device(): lax.all_to_all(outgoing, 'dp', split_axis=0, concat_axis=0, tiled=True)]
    all_gather x2, waiting for transfers between devices: 52.6 us -> 23.5 us  [gather(): return lax.all_gather(piece, 'dp', axis=0, tiled=True)]
    slice x16 -> x0, local copies, waits for them, and re-layouts: 17.8 us -> none  [the longest x12 11.8 us: gather_groups(): right_more[:rows]]
  transfers between devices with their start and end apart: 121 -> 126, of which waited for: 59 -> 66; matrix products, arithmetic and copies ran while one was open for 37% -> 30% of each run, Pallas kernels for 4% -> 5%
where the time goes in v2:
time: 1270 us; the launch traced here: 1250 us
  waiting for transfers between devices  499 us (39%)
  matrix products  168 us (13%)
  other arithmetic  161 us (13%)
  starting transfers between devices  154 us (12%)
  local copies, waits for them, and re-layouts  143 us (11%)
  Pallas kernels  99.1 us (8%)
  between operations  28.5 us (2%)
    ppermute x104, waiting for transfers between devices, send(): lax.ppermute(value, 'grp', [(source, source ^ step) for source in sources])  317 us
    ppermute x104, starting transfers between devices, send(): lax.ppermute(value, 'grp', [(source, source ^ step) for source in sources])  135 us
    all_gather x6, waiting for transfers between devices, gather(): return lax.all_gather(value, 'dp', axis=0, tiled=True)  75.5 us
    dot_general x12, matrix products, transposed_left(): lax.dot_general(left, right, (((0,), (0,)), ((), ())), preferred_element_...  46.7 us
    dot_general x11, matrix products, matmul(): return jnp.dot(left, right, preferred_element_type=FULL)  44.2 us
    pallas_call x12, Pallas kernels, gather_groups(): pl.pallas_call(assemble_kernel, out_shape=jax.ShapeDtypeStruct((4 * rows,...  41.3 us
    dot_general x10, matrix products, transposed_right(): lax.dot_general(left, right, (((1,), (1,)), ((), ())), preferred_element_...  40.2 us
    pallas_call x1, Pallas kernels, feed_in_step(): pl.pallas_call(kernel, out_shape=[jax.ShapeDtypeStruct(weights.shape, FUL...  39.6 us
  transfers between devices with their start and end apart: 126, of which 66 were waited for; matrix products, arithmetic and copies ran while one was open for 30% of the time, Pallas kernels for 5%

profile of v2, /device:TPU:0, one launch (start us, length us, event | category | flops | bytes accessed | tf_op | source)
XLA Modules:
  0.0 1251.9 jit_solution(7493598490013993153)
XLA Ops:
  19.1 21.2 %all-gather.25.cloned.1.call-done = bf16[448,1536]{1,0:T(8,128)(2,1)} async-done(((bf16[56,1536]{1,0:T(8,128)(2,1)}), bf16[448,1536]{1,0:T(8,128)(2,1)}) %all-gather.25.cloned.1.call-update) | async-done | bytes 1376272 | tf_op jit(solution)/shard_map/all_gather | solution.py:442
  42.7 18.2 %shard_map.384 = bf16[2,192,2048]{2,1,0:T(8,128)(2,1)} custom-call(s32[1]{0:T(128)} %bitcast.21.group_ref, f32[2,192,7936]{2,1,0:T(8,128)} %w_ref.1, f32[2,192,7936]{2,1,0:T(8,128)} %w_ref.1), custom_call_target="tpu_custom_call" | custom-call | tf_op jit(solution)/shard_map/pallas_call | solution.py:228
  74.2 38.9 %all-gather.27.cloned.1.call-done = bf16[1,1536,2304]{2,1,0:T(8,128)(2,1)} async-done(((bf16[1,192,2304]{2,1,0:T(8,128)(2,1)}), bf16[1,1536,2304]{2,1,0:T(8,128)(2,1)}) %all-gather.27.cloned.1.call-update) | async-done | bytes 7077904 | tf_op jit(solution)/shard_map/all_gather | solution.py:433
  132.9 12.6 %all-gather.13.cloned.1.call-done = bf16[768,1536]{1,0:T(8,128)(2,1)} async-done(((bf16[96,1536]{1,0:T(8,128)(2,1)}), bf16[768,1536]{1,0:T(8,128)(2,1)}) %all-gather.13.cloned.1.call-update) | async-done | bytes 2359312 | tf_op jit(solution)/shard_map/all_gather | solution.py:433
  154.2 8.3 collective-permute-done.one_ref
  165.8 16.0 %collective-permute-done.1.left_ref = bf16[512,768]{1,0:T(8,128)(2,1)} collective-permute-done((bf16[512,768]{1,0:T(8,128)(2,1)S(1)}, bf16[512,768]{1,0:T(8,128)(2,1)}, u32[]{:S(2)}, u32[]{:S(2)}) %collective-permute-start.1) | collective-permute-done | bytes 786464 | tf_op jit(solution)/shard_map/ppermute | solution.py:104
  187.6 23.9 %all-gather.29.cloned.1.call-done = bf16[1,1536,2048]{2,1,0:T(8,128)(2,1)} async-done(((bf16[1,192,2048]{2,1,0:T(8,128)(2,1)}), bf16[1,1536,2048]{2,1,0:T(8,128)(2,1)}) %all-gather.29.cloned.1.call-update) | async-done | bytes 6291472 | tf_op jit(solution)/shard_map/all_gather | solution.py:433
  211.5 9.7 fusion.10
  227.0 23.5 %all-gather.15.cloned.1.call-done = bf16[1024,1536]{1,0:T(8,128)(2,1)} async-done(((bf16[128,1536]{1,0:T(8,128)(2,1)}), bf16[1024,1536]{1,0:T(8,128)(2,1)}) %all-gather.15.cloned.1.call-update) | async-done | bytes 3145744 | tf_op jit(solution)/shard_map/all_gather | solution.py:254
  259.7 16.6 %collective-permute-done.11 = bf16[512,768]{1,0:T(8,128)(2,1)S(1)} collective-permute-done((bf16[512,768]{1,0:T(8,128)(2,1)S(1)}, bf16[512,768]{1,0:T(8,128)(2,1)S(1)}, u32[]{:S(2)}, u32[]{:S(2)}) %collective-permute-start.11) | collective-permute-done | bytes 786464 | tf_op jit(solution)/shard_map/ppermute | solution.py:104
  278.2 9.0 collective-permute-done.12
  317.7 11.1 collective-permute-done.10
  356.1 34.9 %all-to-all-done = bf16[8,144,384]{2,1,0:T(8,128)(2,1)} async-done(((bf16[8,144,384]{2,1,0:T(8,128)(2,1)}), bf16[8,144,384]{2,1,0:T(8,128)(2,1)}, u32[]{:S(2)}, u32[]{:S(2)}) %all-to-all-start) | async-done | bytes 884768 | tf_op jit(solution)/shard_map/all_to_all | solution.py:518
  421.1 21.3 %collective-permute-done.26 = bf16[256,768]{1,0:T(8,128)(2,1)S(1)} collective-permute-done((bf16[256,768]{1,0:T(8,128)(2,1)S(1)}, bf16[256,768]{1,0:T(8,128)(2,1)S(1)}, u32[]{:S(2)}, u32[]{:S(2)}) %collective-permute-start.26) | collective-permute-done | bytes 393248 | tf_op jit(solution)/shard_map/ppermute | solution.py:104
  490.0 17.9 %collective-permute-done.34 = bf16[256,768]{1,0:T(8,128)(2,1)S(1)} collective-permute-done((bf16[256,768]{1,0:T(8,128)(2,1)S(1)}, bf16[256,768]{1,0:T(8,128)(2,1)S(1)}, u32[]{:S(2)}, u32[]{:S(2)}) %collective-permute-start.34) | collective-permute-done | bytes 393248 | tf_op jit(solution)/shard_map/ppermute | solution.py:104
  508.0 9.2 collective-permute-done.36
  560.7 9.4 collective-permute-done.41
  631.2 21.6 %all-to-all-done.1 = bf16[8,144,384]{2,1,0:T(8,128)(2,1)} async-done(((bf16[8,144,384]{2,1,0:T(8,128)(2,1)}), bf16[8,144,384]{2,1,0:T(8,128)(2,1)}, u32[]{:S(2)}, u32[]{:S(2)}) %all-to-all-start.1) | async-done | bytes 884768 | tf_op jit(solution)/shard_map/all_to_all | solution.py:603
  658.8 19.0 %collective-permute-done.48 = bf16[512,768]{1,0:T(8,128)(2,1)S(1)} collective-permute-done((bf16[512,768]{1,0:T(8,128)(2,1)S(1)}, bf16[512,768]{1,0:T(8,128)(2,1)S(1)}, u32[]{:S(2)}, u32[]{:S(2)}) %collective-permute-start.48) | collective-permute-done | bytes 786464 | tf_op jit(solution)/shard_map/ppermute | solution.py:104
  680.6 8.7 collective-permute-done.49
  720.2 14.2 %collective-permute-done.53.left_ref = bf16[512,768]{1,0:T(8,128)(2,1)S(1)} collective-permute-done((bf16[512,768]{1,0:T(8,128)(2,1)}, bf16[512,768]{1,0:T(8,128)(2,1)S(1)}, u32[]{:S(2)}, u32[]{:S(2)}) %collective-permute-start.53) | collective-permute-done | bytes 786464 | tf_op jit(solution)/shard_map/ppermute | solution.py:104
  740.1 12.9 %fusion.58 = (f32[1024,1024]{1,0:T(8,128)}, f32[1024,1024]{1,0:T(8,128)}) fusion(f32[1024,2048]{1,0:T(8,128)} %copy-done.27, bf16[1024,1536]{1,0:T(8,128)(2,1)} %shard_map.386, bf16[1024,1536]{1,0:T(8,128)(2,1)} %all-gather.15.cloned.1.call-done), kind=kOutput, calls=%fused_computation.134 | convolution fusion | flops 3244294144 | bytes 23068672 | tf_op jit(solution)/shard_map/dot_general | solution.py:34
  753.0 11.1 fusion.333
  767.3 12.2 collective-permute-done.56
  781.6 12.1 convolution_convert_fusion.1
  832.0 15.4 %collective-permute-done.64.left_ref = bf16[512,384]{1,0:T(8,128)(2,1)S(1)} collective-permute-done((bf16[512,384]{1,0:T(8,128)(2,1)}, bf16[512,384]{1,0:T(8,128)(2,1)S(1)}, u32[]{:S(2)}, u32[]{:S(2)}) %collective-permute-start.64) | collective-permute-done | bytes 393248 | tf_op jit(solution)/shard_map/ppermute | solution.py:104
  910.4 10.3 concatenate.221
  944.9 16.5 %collective-permute-done.104.left_ref = bf16[256,768]{1,0:T(8,128)(2,1)S(1)} collective-permute-done((bf16[256,768]{1,0:T(8,128)(2,1)S(1)}, bf16[256,768]{1,0:T(8,128)(2,1)S(1)}, u32[]{:S(2)}, u32[]{:S(2)}) %collective-permute-start.104) | collective-permute-done | bytes 393248 | tf_op jit(solution)/shard_map/ppermute | solution.py:104
  1059.4 8.9 collective-permute-done.70.one_ref
  1175.8 39.6 %shard_map.393 = (f32[2,192,7936]{2,1,0:T(8,128)}, f32[2,192,7936]{2,1,0:T(8,128)}, f32[2,192,7936]{2,1,0:T(8,128)}) custom-call(s32[1]{0:T(128)} %bitcast.21.group_ref, f32[3]{0:T(128)} %pad_maximum_fusion.49.scalar_ref, f32[2,192,7936]{2,1,0:T(8,128)} %w_ref.1, f32[2,192,7936]{2,1,0:T(8,128)} %m_ref.1, f32[2,192,7936]{2,1,0:T(8,128)} %v_ref.1, ...), custom_call_target="tpu_custom_call" | custom-call | flops 60948480 | bytes 79233024 | tf_op jit(solution)/shard_map/pallas_call | solution.py:328
  1215.3 13.4 %multiply_subtract_fusion = (f32[2,496,1536]{2,1,0:T(8,128)}, f32[2,496,1536]{2,1,0:T(8,128)}, f32[2,496,1536]{2,1,0:T(8,128)}) fusion(f32[2,496,1536]{2,1,0:T(8,128)} %param.31, f32[]{:T(128)} %bitcast.110, f32[]{:T(128)} %bitcast.109, f32[]{:T(128)} %min.19, bf16[1,496,1536]{2,1,0:T(8,128)(2,1)} %fusion.53, bf16[1,496,1536]{2,1,0:T(8,128)(2,1)} %fusion.55, ...), kind=kLoop, calls=%fused_computation.19 | loop fusion | flops 27426816 | bytes 39616524 | tf_op jit(solution)/shard_map/sub | solution.py:95
  1228.8 11.8 multiply_subtract_fusion.1
  (1046 shorter events, 693.9 us)
Async XLA Ops:
  7.2 33.1 %all-gather.25.cloned.1.call-start = ((), (), s32[]{:S(2)}) async-start(), calls=%async_computation.24 | async-start | bytes 1548288 | tf_op jit(solution)/shard_map/all_gather | solution.py:442
  13.4 99.6 %all-gather.27.cloned.1.call-start = ((), (), s32[]{:S(2)}) async-start(), calls=%async_computation.25 | async-start | bytes 7962624 | tf_op jit(solution)/shard_map/all_gather | solution.py:433
  16.9 128.6 %all-gather.13.cloned.1.call-start = ((), (), s32[]{:S(2)}) async-start(), calls=%async_computation.10 | async-start | bytes 2654208 | tf_op jit(solution)/shard_map/all_gather | solution.py:433
  42.7 168.8 %all-gather.29.cloned.1.call-start = ((), (), s32[]{:S(2)}) async-start(), calls=%async_computation.26 | async-start | bytes 7077888 | tf_op jit(solution)/shard_map/all_gather | solution.py:433
  63.7 186.8 %all-gather.15.cloned.1.call-start = ((), (), s32[]{:S(2)}) async-start(), calls=%async_computation.11 | async-start | bytes 3538944 | tf_op jit(solution)/shard_map/all_gather | solution.py:254
  120.4 213.0 %all-gather.17.cloned.1.call-start = ((), (), s32[]{:S(2)}) async-start(), calls=%async_computation.12 | async-start | bytes 2211840 | tf_op jit(solution)/shard_map/all_gather | solution.py:433
  150.2 262.9 %all-gather.19.cloned.1.call-start = ((), (), s32[]{:S(2)}) async-start(), calls=%async_computation.13 | async-start | bytes 2654208 | tf_op jit(solution)/shard_map/all_gather | solution.py:433
  151.0 299.3 %all-gather.21.cloned.1.call-start = ((), (), s32[]{:S(2)}) async-start(), calls=%async_computation.14 | async-start | bytes 7077888 | tf_op jit(solution)/shard_map/all_gather | solution.py:433
  339.2 51.8 %all-to-all-start = ((bf16[8,144,384]{2,1,0:T(8,128)(2,1)}), bf16[8,144,384]{2,1,0:T(8,128)(2,1)}, u32[]{:S(2)}, u32[]{:S(2)}) async-start(bf16[8,144,384]{2,1,0:T(8,128)(2,1)} %bitcast.354), calls=%async_computation | async-start | bytes 1769472 | tf_op jit(solution)/shard_map/all_to_all | solution.py:518
  343.4 114.1 %all-gather.23.cloned.1.call-start = ((), (), s32[]{:S(2)}) async-start(), calls=%async_computation.15 | async-start | bytes 3538944 | tf_op jit(solution)/shard_map/all_gather | solution.py:254
  353.9 351.3 %reduce-scatter.11.cloned.1.call-start = ((), (), s32[]{:S(2)}) async-start(), calls=%async_computation.17 | async-start | bytes 3538944 | tf_op jit(solution)/shard_map/reduce_scatter | solution.py:436
  418.4 24.0 %collective-permute-start.26 = (bf16[256,768]{1,0:T(8,128)(2,1)S(1)}, bf16[256,768]{1,0:T(8,128)(2,1)S(1)}, u32[]{:S(2)}, u32[]{:S(2)}) collective-permute-start(bf16[256,768]{1,0:T(8,128)(2,1)S(1)} %get-tuple-element.242), channel_id=1, source_target_pairs={{24,8},{16,0},{25,9},{17,1},{26,10},{18,2},{27,11},{19,3},{28,12},... | collective-permute-start | bytes 1179656 | tf_op jit(solution)/shard_map/ppermute | solution.py:104
  419.8 30.4 %collective-permute-start.28 = (bf16[256,768]{1,0:T(8,128)(2,1)S(1)}, bf16[256,768]{1,0:T(8,128)(2,1)S(1)}, u32[]{:S(2)}, u32[]{:S(2)}) collective-permute-start(bf16[256,768]{1,0:T(8,128)(2,1)S(1)} %broadcast_select_fusion.2), channel_id=1, source_target_pairs={{24,16},{8,0},{25,17},{9,1},{26,18},{10,2},{27,19},{11,3},{28,20},... | collective-permute-start | bytes 1179656 | tf_op jit(solution)/shard_map/ppermute | solution.py:104
  488.2 29.0 %collective-permute-start.36 = (bf16[256,768]{1,0:T(8,128)(2,1)S(1)}, bf16[256,768]{1,0:T(8,128)(2,1)S(1)}, u32[]{:S(2)}, u32[]{:S(2)}) collective-permute-start(bf16[256,768]{1,0:T(8,128)(2,1)S(1)} %broadcast_select_fusion), channel_id=1, source_target_pairs={{24,16},{8,0},{25,17},{9,1},{26,18},{10,2},{27,19},{11,3},{28,20},... | collective-permute-start | bytes 1179656 | tf_op jit(solution)/shard_map/ppermute | solution.py:104
  548.4 156.9 %reduce-scatter.9.cloned.1.call-start = ((), (), s32[]{:S(2)}) async-start(), calls=%async_computation.16 | async-start | bytes 7077888 | tf_op jit(solution)/shard_map/reduce_scatter | solution.py:436
  610.8 42.0 %all-to-all-start.1 = ((bf16[8,144,384]{2,1,0:T(8,128)(2,1)}), bf16[8,144,384]{2,1,0:T(8,128)(2,1)}, u32[]{:S(2)}, u32[]{:S(2)}) async-start(bf16[8,144,384]{2,1,0:T(8,128)(2,1)} %bitcast.355), calls=%async_computation.1 | async-start | bytes 1769472 | tf_op jit(solution)/shard_map/all_to_all | solution.py:603
  615.1 193.9 %reduce-scatter.15.cloned.1.call-start = ((), (), s32[]{:S(2)}) async-start(), calls=%async_computation.19 | async-start | bytes 2654208 | tf_op jit(solution)/shard_map/reduce_scatter | solution.py:436
  679.2 129.8 %reduce-scatter.13.cloned.1.call-start = ((), (), s32[]{:S(2)}) async-start(), calls=%async_computation.18 | async-start | bytes 4423680 | tf_op jit(solution)/shard_map/reduce_scatter | solution.py:436
  720.2 200.5 %reduce-scatter.19.cloned.1.call-start = ((), (), s32[]{:S(2)}) async-start(), calls=%async_computation.21 | async-start | bytes 3538944 | tf_op jit(solution)/shard_map/reduce_scatter | solution.py:436
  766.6 27.1 %collective-permute-start.58 = (bf16[512,768]{1,0:T(8,128)(2,1)}, bf16[512,768]{1,0:T(8,128)(2,1)}, u32[]{:S(2)}, u32[]{:S(2)}) collective-permute-start(bf16[512,768]{1,0:T(8,128)(2,1)} %pad_maximum_fusion.25), channel_id=1, source_target_pairs={{0,8},{8,0},{16,24},{24,16},{1,9},{9,1},{17,25},{25,17},{2,10},{10... | collective-permute-start | bytes 2359304 | tf_op jit(solution)/shard_map/ppermute | solution.py:104
  809.0 112.0 %reduce-scatter.17.cloned.1.call-start = ((), (), s32[]{:S(2)}) async-start(), calls=%async_computation.20 | async-start | bytes 7077888 | tf_op jit(solution)/shard_map/reduce_scatter | solution.py:436
  809.6 212.0 %reduce-scatter.21.cloned.1.call-start = ((), (), s32[]{:S(2)}) async-start(), calls=%async_computation.22 | async-start | bytes 10616832 | tf_op jit(solution)/shard_map/reduce_scatter | solution.py:436
  821.1 31.7 %collective-permute-start.5 = (bf16[512,768]{1,0:T(8,128)(2,1)}, bf16[512,768]{1,0:T(8,128)(2,1)}, u32[]{:S(2)}, u32[]{:S(2)}) collective-permute-start(bf16[512,768]{1,0:T(8,128)(2,1)} %pad_maximum_fusion.17), channel_id=1, source_target_pairs={{0,16},{8,24},{16,0},{24,8},{1,17},{9,25},{17,1},{25,9},{2,18},{10... | collective-permute-start | bytes 2359304 | tf_op jit(solution)/shard_map/ppermute | solution.py:104
  825.4 27.4 %collective-permute-start.7 = (bf16[512,768]{1,0:T(8,128)(2,1)}, bf16[512,768]{1,0:T(8,128)(2,1)}, u32[]{:S(2)}, u32[]{:S(2)}) collective-permute-start(bf16[512,768]{1,0:T(8,128)(2,1)} %pad_maximum_fusion.18), channel_id=1, source_target_pairs={{0,8},{8,0},{16,24},{24,16},{1,9},{9,1},{17,25},{25,17},{2,10},{10... | collective-permute-start | bytes 2359304 | tf_op jit(solution)/shard_map/ppermute | solution.py:104
  921.0 197.4 %reduce-scatter.23.cloned.1.call-start = ((), (), s32[]{:S(2)}) async-start(), calls=%async_computation.23 | async-start | bytes 3096576 | tf_op jit(solution)/shard_map/reduce_scatter | solution.py:436
  934.0 31.6 %collective-permute-start.96 = (bf16[384,1024]{1,0:T(8,128)(2,1)}, bf16[384,1024]{1,0:T(8,128)(2,1)}, u32[]{:S(2)}, u32[]{:S(2)}) collective-permute-start(bf16[384,1024]{1,0:T(8,128)(2,1)} %pad_maximum_fusion.30), channel_id=1, source_target_pairs={{0,16},{8,24},{16,0},{24,8},{1,17},{9,25},{17,1},{25,9},{2,18},{10... | collective-permute-start | bytes 2359304 | tf_op jit(solution)/shard_map/ppermute | solution.py:104
  936.6 29.1 %collective-permute-start.98 = (bf16[384,1024]{1,0:T(8,128)(2,1)}, bf16[384,1024]{1,0:T(8,128)(2,1)}, u32[]{:S(2)}, u32[]{:S(2)}) collective-permute-start(bf16[384,1024]{1,0:T(8,128)(2,1)} %pad_maximum_fusion.31), channel_id=1, source_target_pairs={{0,8},{8,0},{16,24},{24,16},{1,9},{9,1},{17,25},{25,17},{2,10},{10... | collective-permute-start | bytes 2359304 | tf_op jit(solution)/shard_map/ppermute | solution.py:104
  1044.9 23.5 %collective-permute-start.70 = (f32[192,768]{1,0:T(8,128)S(1)}, f32[192,768]{1,0:T(8,128)S(1)}, u32[]{:S(2)}, u32[]{:S(2)}) collective-permute-start(f32[192,768]{1,0:T(8,128)S(1)} %get-tuple-element.210), channel_id=1, source_target_pairs={{0,8},{8,0},{16,24},{24,16},{1,9},{9,1},{17,25},{25,17},{2,10},{10... | collective-permute-start | bytes 1769480 | tf_op jit(solution)/shard_map/ppermute | solution.py:104
  1055.8 31.9 %collective-permute-start.92 = (bf16[384,1024]{1,0:T(8,128)(2,1)S(1)}, bf16[384,1024]{1,0:T(8,128)(2,1)S(1)}, u32[]{:S(2)}, u32[]{:S(2)}) collective-permute-start(bf16[384,1024]{1,0:T(8,128)(2,1)S(1)} %pad_maximum_fusion.28), channel_id=1, source_target_pairs={{0,16},{8,24},{16,0},{24,8},{1,17},{9,25},{17,1},{25,9},{2,18},{10... | collective-permute-start | bytes 2359304 | tf_op jit(solution)/shard_map/ppermute | solution.py:104
  1058.2 30.3 %collective-permute-start.94 = (bf16[384,1024]{1,0:T(8,128)(2,1)S(1)}, bf16[384,1024]{1,0:T(8,128)(2,1)}, u32[]{:S(2)}, u32[]{:S(2)}) collective-permute-start(bf16[384,1024]{1,0:T(8,128)(2,1)S(1)} %pad_maximum_fusion.29), channel_id=1, source_target_pairs={{0,8},{8,0},{16,24},{24,16},{1,9},{9,1},{17,25},{25,17},{2,10},{10... | collective-permute-start | bytes 2359304 | tf_op jit(solution)/shard_map/ppermute | solution.py:104
  1069.5 37.6 %collective-permute-start.71 = (f32[384,768]{1,0:T(8,128)}, f32[384,768]{1,0:T(8,128)}, u32[]{:S(2)}, u32[]{:S(2)}) collective-permute-start(f32[384,768]{1,0:T(8,128)} %pad_maximum_fusion.13), channel_id=1, source_target_pairs={{0,16},{8,24},{16,0},{24,8},{1,17},{9,25},{17,1},{25,9},{2,18},{10... | collective-permute-start | bytes 3538952 | tf_op jit(solution)/shard_map/ppermute | solution.py:104
  1072.1 35.0 %collective-permute-start.73 = (f32[384,768]{1,0:T(8,128)}, f32[384,768]{1,0:T(8,128)}, u32[]{:S(2)}, u32[]{:S(2)}) collective-permute-start(f32[384,768]{1,0:T(8,128)} %pad_maximum_fusion.14), channel_id=1, source_target_pairs={{0,8},{8,0},{16,24},{24,16},{1,9},{9,1},{17,25},{25,17},{2,10},{10... | collective-permute-start | bytes 3538952 | tf_op jit(solution)/shard_map/ppermute | solution.py:104
  (314 other events, 2851.2 us)
Sparse Core Ops, SparseCore 0:
  13.6 26.6 all-gather.24
  42.5 70.5 all-gather.26
  115.3 30.1 all-gather.12
  147.6 63.8 all-gather.28
  213.6 36.9 all-gather.14
  252.6 26.8 all-gather.16
  281.7 31.1 all-gather.18
  315.1 82.5 all-gather.20
  399.9 36.8 all-gather.22
  548.5 42.5 reduce-scatter.10
  594.0 83.1 reduce-scatter.8
  679.9 38.5 reduce-scatter.14
  721.4 46.6 reduce-scatter.12
  809.1 40.1 reduce-scatter.18
  852.0 68.8 reduce-scatter.16
  923.7 97.8 reduce-scatter.20
  1024.3 36.4 reduce-scatter.22
